TPU v7x, 32 devices: a whole 2x2x4 slice. The times are simulated.
32 devices in a mesh: dp: 8 (over z, y), pipe: 2 (over x), tensor: 2 (over core).
Axes of the slice: x: 2, y: 2, z: 4, core: 2. Of those that a mesh axis runs over, the one named last changes fastest.
Arguments:
- hidden: bfloat16 [2, 1024, 8192], P('pipe', 'dp', 'tensor'), may hold values from -6 to 6
- doc_lengths: int32 [2, 8, 8], P('pipe', 'dp'), may hold values from 1 to 32, 128 in all within a row
- doc_target: int32 [2, 8, 8], P('pipe', 'dp'), may hold values from 0 to 7, each once within a row
- norm_gain: float32 [2, 8192], P('pipe'), may hold values from 0.5 to 1.5
- q_weight: bfloat16 [2, 8192, 8192], P('pipe', None, 'tensor'), may hold values from -0.0625 to 0.0625
- kv_weight: bfloat16 [2, 8192, 2048], P('pipe', None, 'tensor'), may hold values from -0.0625 to 0.0625
Outputs:
- balanced: bfloat16 [2, 2048, 8192], P('pipe', 'dp', 'tensor')
Inputs may be any that keep to these rules, and one draw needn't show every extreme that they name: `doc_lengths`: each row of lengths sums to 128 and its largest entry is exactly 32. `doc_target`: each row is a permutation of the dp indices.
All inputs are finite; a program needn't handle non-finite values.
Results may differ from a plain program's by a relative error of at most 0.0067.
Values may be sent and summed in bfloat16 or wider, within the bound.
A program may use at most 128 MiB of HBM per device.

v0:
```python
import functools

import jax
import jax.numpy as jnp
from jax import lax
from jax.experimental import pallas as pl
from jax.experimental.pallas import tpu as pltpu
from jax.sharding import PartitionSpec as P

D = 8192
HD = 128
KV_HEADS = 8
STEPS = 2


def passed_along(block, axis, distance):
    devices = range(lax.axis_size(axis))
    route = [((i - distance) % len(devices), i) for i in devices]
    return lax.ppermute(block, axis, route)


def build_send(token_rows, lengths, targets, capacity, groups):
    ordinal = jnp.arange(groups, dtype=jnp.int32)
    offsets = jnp.cumsum(lengths) - lengths
    onehot = (targets[None, :] == ordinal[:, None]).astype(jnp.int32)
    doc_sizes = jnp.sum(onehot * lengths[None, :], axis=1)
    doc_starts = jnp.sum(onehot * offsets[None, :], axis=1)
    within = jnp.arange(capacity, dtype=jnp.int32)
    row_index = jnp.minimum(doc_starts[:, None] + within[None, :], token_rows.shape[0] - 1)
    picked = jnp.take(token_rows, row_index.reshape(-1), axis=0).reshape(
        groups, capacity, token_rows.shape[1]
    )
    inside = within[None, :] < doc_sizes[:, None]
    return (jnp.where(inside[:, :, None], picked, jnp.zeros_like(picked)), doc_sizes)


def doc_masks(lengths, length):
    within = jnp.arange(length, dtype=jnp.int32)
    doc_ends = jnp.cumsum(lengths)
    segment = jnp.sum((within[:, None] >= doc_ends[None, :]).astype(jnp.int32), axis=1)
    causal = within[:, None] >= within[None, :]
    return (segment[:, None] == segment[None, :]) & causal


def attend_heads(queries, kv_local, allowed, local_rank):
    row_count = queries.shape[0]
    local_heads = queries.shape[1] // HD
    per_group = D // HD // KV_HEADS
    kv_count = max(1, local_heads // per_group)
    kv_first = local_rank * local_heads // per_group
    kv_whole = lax.all_gather(kv_local, "tensor", axis=1, tiled=True)
    kv_heads = kv_whole.reshape(row_count, 2, HD, KV_HEADS)
    own_heads = lax.dynamic_slice_in_dim(kv_heads, kv_first, kv_count, 3)
    key_rows = own_heads[:, 0]
    values = own_heads[:, 1]
    grouped = queries.reshape(row_count, kv_count, local_heads // kv_count, HD)
    scores = jnp.einsum(
        "qcph,khc->cpqk", grouped, key_rows, preferred_element_type=jnp.float32
    ) * HD ** (-0.5)
    exp_scores = jnp.where(allowed[None, None], jnp.exp(scores), 0.0)
    probabilities = (exp_scores / jnp.sum(exp_scores, axis=-1, keepdims=True)).astype(jnp.bfloat16)
    attended = jnp.einsum(
        "cpqk,khc->qcph", probabilities, values, preferred_element_type=jnp.float32
    )
    return attended.reshape(row_count, queries.shape[1])


def layer_pass(current, gain_full, query_cols, kv_cols, allowed):
    local_rank = lax.axis_index("tensor")
    widened = current.astype(jnp.float32)
    whole = lax.all_gather(current, "tensor", axis=1, tiled=True)
    whole_wide = whole.astype(jnp.float32)
    scale_row = lax.rsqrt(jnp.sum(whole_wide * whole_wide, axis=-1) / D + 1e-05)
    normed_full = (whole_wide * scale_row[:, None] * gain_full).astype(jnp.bfloat16)
    query_sum = jnp.dot(normed_full, query_cols, preferred_element_type=jnp.float32)
    kv_sum = jnp.dot(normed_full, kv_cols, preferred_element_type=jnp.float32)
    queries = query_sum.astype(jnp.bfloat16)
    kv_local = kv_sum.astype(jnp.bfloat16)
    attended = attend_heads(queries, kv_local, allowed, local_rank)
    return (widened + attended).astype(jnp.bfloat16)


def on_device(hidden, doc_lengths, doc_target, norm_gain, q_weight, kv_weight):
    groups = lax.axis_size("dp")
    current = hidden[0]
    lengths = doc_lengths[0, 0]
    targets = doc_target[0, 0]
    capacity = current.shape[0] // 4
    gain_full = norm_gain[0]
    query_cols = q_weight[0]
    kv_cols = kv_weight[0]
    carried = jnp.stack([lengths, targets]).astype(jnp.bfloat16)
    for layer_step in range(STEPS):
        allowed = doc_masks(carried[0].astype(jnp.int32), current.shape[0])
        current = layer_pass(current, gain_full, query_cols, kv_cols, allowed)
        if layer_step + 1 < STEPS:
            current, carried = passed_along((current, carried), "pipe", 1)
    final_lengths = carried[0].astype(jnp.int32)
    final_targets = carried[1].astype(jnp.int32)
    packed, doc_sizes = build_send(current, final_lengths, final_targets, capacity, groups)
    received = lax.all_to_all(packed, "dp", split_axis=0, concat_axis=0, tiled=True)
    return received.reshape(1, groups * capacity, received.shape[2])


CHUNK = 256
SLOTS = 6


def split_masks(n_dp):
    early = [m for m in range(n_dp) if m >= n_dp // 2 and m % 2 == 0]
    return early, [m for m in range(n_dp) if m not in early]


def fused_kernel(
    sizes, hidden, lengths, targets, gain, wq, wkv, out, meta,
    x_own, x_other, h_send, next_own, next_other, early_own, early_other, early_send,
    meta_next, meta_early, normed, spread, kv_cols,
    kv_send, kv_heads, kv_weights, ring, mask, early_mask, valid, early_chooser, late_chooser,
    q_held, packed, early_out,
    sem_x, sem_xs, sem_xr, sem_ms, sem_mr, sem_kvw, sem_ring, sem_kvs, sem_kvr,
    sem_hs, sem_hr, sem_fs, sem_fr, sem_as, sem_ar, sem_own,
    sem_es, sem_er, sem_gs, sem_gr, sem_mes, sem_mer,
):
    n_dp, n_pipe, docs = sizes
    rows, width = hidden.shape
    features = gain.shape[1]
    n_chunks = width // CHUNK
    kv_chunks = wkv.shape[1] // CHUNK
    own_kv = kv_heads.shape[2]
    chunk_heads = CHUNK // HD
    group_chunks = n_chunks // own_kv
    capacity = packed.shape[1]
    early_masks, late_masks = split_masks(n_dp)
    half = len(early_masks)
    early_rows = half * capacity
    dp = lax.axis_index("dp")
    pipe = lax.axis_index("pipe")
    side = lax.axis_index("tensor")
    other = 1 - side
    following = lax.rem(pipe + 1, n_pipe)
    preceding = lax.rem(pipe + n_pipe - 1, n_pipe)
    total = STEPS * n_chunks
    layer_rows = (rows, rows + early_rows)

    def partner(flips):
        index, bit = dp, 1
        while bit < n_dp:
            if flips & bit:
                index = index + bit - 2 * bit * lax.rem(dp // bit, 2)
            bit *= 2
        return index

    early_partners = [partner(m) for m in early_masks]
    late_partners = [partner(m) for m in late_masks]

    def cols(j):
        return pl.ds(pl.multiple_of(j * CHUNK, CHUNK), CHUNK)

    def kv_copy(n):
        return pltpu.make_async_copy(wkv.at[:, cols(n)], kv_weights.at[n], sem_kvw.at[n])

    def ring_copy(c):
        slot = lax.rem(c, SLOTS)
        return pltpu.make_async_copy(
            wq.at[:, cols(lax.rem(c, n_chunks))], ring.at[slot], sem_ring.at[slot]
        )

    def x_copy(j):
        return pltpu.make_async_copy(hidden.at[:, cols(j)], x_own.at[j], sem_x.at[j])

    def x_remote(j):
        return pltpu.make_async_remote_copy(
            hidden.at[:, cols(j)], x_other.at[j], sem_xs.at[j], sem_xr.at[j],
            device_id={"tensor": other}, device_id_type=pl.DeviceIdType.MESH,
        )

    def meta_remote():
        return pltpu.make_async_remote_copy(
            meta, meta_next, sem_ms, sem_mr,
            device_id={"pipe": following}, device_id_type=pl.DeviceIdType.MESH,
        )

    def meta_on(k):
        return pltpu.make_async_remote_copy(
            meta_next, meta_early.at[k], sem_mes.at[k], sem_mer.at[k],
            device_id={"dp": early_partners[k]}, device_id_type=pl.DeviceIdType.MESH,
        )

    def early_remote(k, j):
        return pltpu.make_async_remote_copy(
            early_send.at[j, k], early_own.at[j, k * capacity:(k + 1) * capacity],
            sem_es.at[k, j], sem_er.at[k, j],
            device_id={"dp": early_partners[k]}, device_id_type=pl.DeviceIdType.MESH,
        )

    def early_forward(j):
        return pltpu.make_async_remote_copy(
            early_own.at[j], early_other.at[j], sem_gs.at[j], sem_gr.at[j],
            device_id={"tensor": other}, device_id_type=pl.DeviceIdType.MESH,
        )

    def kv_remote(layer):
        here = pl.ds(0, layer_rows[layer])
        return pltpu.make_async_remote_copy(
            kv_send.at[layer, :, here], kv_heads.at[layer, side, :, here], sem_kvs.at[layer], sem_kvr.at[layer],
            device_id={"tensor": other}, device_id_type=pl.DeviceIdType.MESH,
        )

    def h_remote(j):
        return pltpu.make_async_remote_copy(
            h_send.at[j], next_own.at[j], sem_hs.at[j], sem_hr.at[j],
            device_id={"pipe": following}, device_id_type=pl.DeviceIdType.MESH,
        )

    def forward_remote(j):
        return pltpu.make_async_remote_copy(
            next_own.at[j], next_other.at[j], sem_fs.at[j], sem_fr.at[j],
            device_id={"tensor": other}, device_id_type=pl.DeviceIdType.MESH,
        )

    def doc_rows(index):
        return pl.ds(pl.multiple_of(index * capacity, capacity), capacity)

    def doc_remote(k, j):
        return pltpu.make_async_remote_copy(
            packed.at[k, :, cols(j)], out.at[doc_rows(dp), cols(j)],
            sem_as.at[k], sem_ar.at[k],
            device_id={"dp": late_partners[k]}, device_id_type=pl.DeviceIdType.MESH,
        )

    def doc_all(k):
        return pltpu.make_async_remote_copy(
            packed.at[k], out.at[doc_rows(late_partners[k])],
            sem_as.at[k], sem_ar.at[k],
            device_id={"dp": late_partners[k]}, device_id_type=pl.DeviceIdType.MESH,
        )

    def own_store(j):
        return pltpu.make_async_copy(
            packed.at[0, :, cols(j)], out.at[doc_rows(dp), cols(j)], sem_own.at[half]
        )

    def own_stored():
        return pltpu.make_async_copy(packed.at[0], out.at[doc_rows(dp)], sem_own.at[half])

    def early_store(k, j):
        return pltpu.make_async_copy(
            early_out.at[k, :, cols(j)], out.at[doc_rows(early_partners[k]), cols(j)],
            sem_own.at[k],
        )

    def early_stored(k):
        return pltpu.make_async_copy(
            early_out.at[k], out.at[doc_rows(early_partners[k])], sem_own.at[k]
        )

    for j in range(n_chunks):
        x_copy(j).start()
    for n in range(kv_chunks):
        kv_copy(n).start()
    for c in range(SLOTS):
        ring_copy(c).start()

    meta[...] = jnp.zeros(meta.shape, jnp.int32)
    meta[0:1, 0:docs] = lengths[...]
    meta[1:2, 0:docs] = targets[...]
    barrier = pltpu.get_barrier_semaphore()
    pl.semaphore_signal(
        barrier, inc=1, device_id={"tensor": other}, device_id_type=pl.DeviceIdType.MESH
    )
    pl.semaphore_signal(
        barrier, inc=1, device_id={"pipe": following}, device_id_type=pl.DeviceIdType.MESH
    )
    greeted = n_dp + 1
    if n_pipe > 2:
        pl.semaphore_signal(
            barrier, inc=1, device_id={"pipe": preceding}, device_id_type=pl.DeviceIdType.MESH
        )
        greeted += 1
    for away in range(1, n_dp):
        pl.semaphore_signal(
            barrier, inc=1, device_id={"dp": lax.rem(dp + away, n_dp)},
            device_id_type=pl.DeviceIdType.MESH,
        )
    pl.semaphore_wait(barrier, greeted)
    for j in range(n_chunks):
        x_remote(j).start()
    meta_remote().start()

    n_kv = kv_cols.shape[1]
    cols_wide = spread.shape[0]
    out_col = lax.broadcasted_iota(jnp.int32, (128, n_kv), 1)
    wanted = lax.rem(out_col, HD) * KV_HEADS + out_col // HD

    def fill_spread(i, carry):
        base = pl.multiple_of(i * 128, 128)
        row = lax.broadcasted_iota(jnp.int32, (128, n_kv), 0) + base
        spread[pl.ds(base, 128), :] = (row == wanted).astype(jnp.float32).astype(jnp.bfloat16)
        return carry

    lax.fori_loop(0, cols_wide // 128, fill_spread, 0)

    def fill_mask(source):
        row = lax.broadcasted_iota(jnp.int32, (rows, rows), 0)
        col = lax.broadcasted_iota(jnp.int32, (rows, rows), 1)
        row_doc = jnp.zeros((rows, rows), jnp.int32)
        col_doc = jnp.zeros((rows, rows), jnp.int32)
        end = jnp.zeros((1, 1), jnp.int32)
        for d in range(docs):
            end = end + source[0:1, d:d + 1]
            row_doc = row_doc + (row >= end).astype(jnp.int32)
            col_doc = col_doc + (col >= end).astype(jnp.int32)
        allowed = jnp.where((row_doc == col_doc) & (row >= col), 1.0, 0.0)
        for i in range(chunk_heads):
            mask[i * rows:(i + 1) * rows, :] = allowed

    def fill_early_mask():
        row = lax.broadcasted_iota(jnp.int32, (early_rows, early_rows), 0)
        col = lax.broadcasted_iota(jnp.int32, (early_rows, early_rows), 1)
        allowed = jnp.where((row // capacity == col // capacity) & (row >= col), 1.0, 0.0)
        for i in range(chunk_heads):
            early_mask[i * early_rows:(i + 1) * early_rows, :] = allowed

    def fill_valid():
        row = lax.broadcasted_iota(jnp.int32, (capacity, CHUNK), 0)
        for slot in range(half):
            size = jnp.zeros((1, 1), jnp.int32)
            for d in range(docs):
                here = meta_early[slot, 1:2, d:d + 1] == dp
                size = size + jnp.where(here, meta_early[slot, 0:1, d:d + 1], 0)
            valid[slot * capacity:(slot + 1) * capacity, :] = jnp.where(row < size, 1.0, 0.0)

    def fill_choosers(source):
        row = lax.broadcasted_iota(jnp.int32, (1, rows), 1)
        goals = [jnp.full((1, rows), -1, jnp.int32) for _ in range(2)]
        begin = jnp.zeros((1, 1), jnp.int32)
        for d in range(docs):
            end = begin + source[0:1, d:d + 1]
            target = source[1:2, d:d + 1]
            inside = (row >= begin) & (row < end)
            for i, partners in enumerate((early_partners, late_partners)):
                first = jnp.full((1, 1), -n_dp * capacity, jnp.int32)
                for k, index in enumerate(partners):
                    first = jnp.where(target == index, k * capacity, first)
                goals[i] = jnp.where(inside, first + row - begin, goals[i])
            begin = end
        for ref, goal in zip((early_chooser, late_chooser), goals):
            slot = lax.broadcasted_iota(jnp.int32, ref.shape, 0)
            ref[...] = (slot == goal).astype(jnp.float32).astype(jnp.bfloat16)

    def normalise(mine, theirs, first, count):
        held_rows = pl.ds(first, count)

        def squares(j, acc):
            a = mine[j].astype(jnp.float32)
            b = theirs[j].astype(jnp.float32)
            return acc + a * a + b * b

        acc = lax.fori_loop(0, n_chunks, squares, jnp.zeros((count, CHUNK), jnp.float32))
        scale = lax.rsqrt(jnp.sum(acc, axis=-1, keepdims=True) / features + 1e-05)

        def write(j, carry):
            for held, half in ((mine, side), (theirs, other)):
                where = cols(half * n_chunks + j)
                wide = held[j].astype(jnp.float32) * scale * gain[:, where]
                normed[held_rows, where] = wide.astype(jnp.bfloat16)
            return carry

        lax.fori_loop(0, n_chunks, write, 0)

    def keys_values(layer):
        count = layer_rows[layer]

        def one(n, carry):
            if layer == 0:
                kv_copy(n).wait()
            kv_cols[0:count, cols(n)] = jnp.dot(
                normed[0:count, :], kv_weights[n], preferred_element_type=jnp.float32
            ).astype(jnp.bfloat16)
            return carry

        lax.fori_loop(0, kv_chunks, one, 0)
        for which, keep in ((other, False), (side, True)):
            first = pl.multiple_of(which * own_kv * HD, own_kv * HD)
            heads = jnp.dot(
                kv_cols[0:count, :], spread[:, pl.ds(first, own_kv * HD)],
                preferred_element_type=jnp.float32,
            ).astype(jnp.bfloat16)
            for g in range(own_kv):
                if keep:
                    kv_heads[layer, side, g, 0:count] = heads[:, g * HD:(g + 1) * HD]
                else:
                    kv_send[layer, g, 0:count] = heads[:, g * HD:(g + 1) * HD]
            if not keep:
                kv_remote(layer).start()

    def query(layer, c):
        return jnp.dot(
            normed[0:layer_rows[layer], :], ring[lax.rem(c, SLOTS)], preferred_element_type=jnp.float32
        ).astype(jnp.bfloat16)

    def attend(layer, j, mine, first, count, allowed):
        here = slice(first, first + count)
        q = q_held[lax.rem(j, 2), here]
        g = j // group_chunks
        stacked = jnp.concatenate([q[:, i * HD:(i + 1) * HD] for i in range(chunk_heads)], axis=0)
        scores = lax.dot_general(
            stacked, kv_heads[layer, 0, g, here], (((1,), (1,)), ((), ())),
            preferred_element_type=jnp.float32,
        ) * HD ** (-0.5)
        e = jnp.where(allowed[...] > 0.0, jnp.exp(scores), 0.0)
        p = (e * (1.0 / jnp.sum(e, axis=-1, keepdims=True))).astype(jnp.bfloat16)
        a = jnp.dot(p, kv_heads[layer, 1, g, here], preferred_element_type=jnp.float32)
        side_by_side = jnp.concatenate(
            [a[i * count:(i + 1) * count] for i in range(chunk_heads)], axis=1
        )
        return (mine[j].astype(jnp.float32) + side_by_side).astype(jnp.bfloat16)

    def attend_all(layer, j):
        if layer == 0:
            return (attend(0, j, x_own, 0, rows, mask),)
        return (
            attend(1, j, next_own, 0, rows, mask),
            attend(1, j, early_own, rows, early_rows, early_mask),
        )

    def refill(c):
        @pl.when(c + SLOTS < total)
        def _():
            ring_copy(c + SLOTS).start()

    def run_layer(layer, finish):
        count = layer_rows[layer]
        base = layer * n_chunks
        ring_copy(base).wait()
        q_held[0, 0:count] = query(layer, base)
        refill(jnp.int32(base))
        kv_remote(layer).wait()

        def one(j, carry):
            c = base + j
            ring_copy(c).wait()
            fresh = query(layer, c)
            done = attend_all(layer, j - 1)
            q_held[lax.rem(j, 2), 0:count] = fresh
            refill(c)
            finish(j - 1, *done)
            return carry

        lax.fori_loop(1, n_chunks, one, 0)
        finish(n_chunks - 1, *attend_all(layer, n_chunks - 1))

    lag, early_lag = 4, 7

    def pass_on(j):
        h_remote(j).wait_recv()
        forward_remote(j).start()
        picked = jnp.dot(
            early_chooser[...], next_own[j], preferred_element_type=jnp.float32
        ).astype(jnp.bfloat16)
        for slot in range(half):
            early_send[j, slot] = picked[slot * capacity:(slot + 1) * capacity]
        for k in range(half):
            early_remote(k, j).start()

    def pass_early(j):
        for k in range(half):
            early_remote(k, j).wait_recv()
        early_forward(j).start()

    def send_next(j, done):
        h_send[j] = done
        h_remote(j).start()

        @pl.when(j >= lag)
        def _():
            pass_on(j - lag)

        @pl.when(j >= early_lag)
        def _():
            pass_early(j - early_lag)

    def send_docs(j, done, early):
        picked = jnp.dot(late_chooser[...], done, preferred_element_type=jnp.float32)
        picked = picked.astype(jnp.bfloat16)
        kept = jnp.where(valid[...] > 0.0, early.astype(jnp.float32), 0.0).astype(jnp.bfloat16)
        for slot in range(len(late_masks)):
            packed[slot, :, cols(j)] = picked[slot * capacity:(slot + 1) * capacity]
        for k in reversed(range(1, len(late_masks))):
            doc_remote(k, j).start()
        own_store(j).start()
        for slot in range(half):
            early_out[slot, :, cols(j)] = kept[slot * capacity:(slot + 1) * capacity]
        for slot in range(half):
            early_store(slot, j).start()

    fill_mask(meta)
    fill_early_mask()
    meta_remote().wait()
    for k in range(half):
        meta_on(k).start()
    fill_choosers(meta_next)
    for j in range(n_chunks):
        x_copy(j).wait()
    for j in range(n_chunks):
        x_remote(j).wait()
    normalise(x_own, x_other, 0, rows)
    keys_values(0)
    run_layer(0, send_next)
    for j in range(n_chunks - lag, n_chunks):
        pass_on(j)
    fill_mask(meta_next)
    for k in range(half):
        meta_on(k).wait()
    fill_valid()
    for j in range(n_chunks - early_lag, n_chunks):
        pass_early(j)
    for j in range(n_chunks):
        forward_remote(j).wait()
    normalise(next_own, next_other, 0, rows)
    for j in range(n_chunks):
        early_forward(j).wait()
    normalise(early_own, early_other, rows, early_rows)
    keys_values(1)
    run_layer(1, send_docs)
    for j in range(n_chunks):
        h_remote(j).wait_send()
        for k in range(half):
            early_remote(k, j).wait_send()
    for slot in range(half):
        early_stored(slot).wait()
    own_stored().wait()
    for k in range(1, len(late_masks)):
        doc_all(k).wait()


def fused_device(sizes, hidden, doc_lengths, doc_target, norm_gain, q_weight, kv_weight):
    n_dp, n_pipe, docs = sizes
    rows, width = hidden.shape[1:]
    features = norm_gain.shape[1]
    n_chunks = width // CHUNK
    n_kv = kv_weight.shape[2]
    kv_chunks = n_kv // CHUNK
    own_kv = KV_HEADS // 2
    capacity = rows // 4
    chunk_heads = CHUNK // HD
    bf16 = jnp.bfloat16
    dma = pltpu.SemaphoreType.DMA
    vmem = pltpu.VMEM
    early_masks, late_masks = split_masks(n_dp)
    half, n_late = len(early_masks), len(late_masks)
    early_rows = half * capacity
    most = rows + early_rows
    blocks = vmem((n_chunks, rows, CHUNK), bf16)
    early_blocks = vmem((n_chunks, early_rows, CHUNK), bf16)
    result = pl.pallas_call(
        functools.partial(fused_kernel, sizes),
        out_shape=jax.ShapeDtypeStruct((n_dp * capacity, width), bf16),
        in_specs=[
            pl.BlockSpec(memory_space=pl.ANY),
            pl.BlockSpec(memory_space=pltpu.VMEM),
            pl.BlockSpec(memory_space=pltpu.VMEM),
            pl.BlockSpec(memory_space=pltpu.VMEM),
            pl.BlockSpec(memory_space=pl.ANY),
            pl.BlockSpec(memory_space=pl.ANY),
        ],
        out_specs=pl.BlockSpec(memory_space=pl.ANY),
        scratch_shapes=[
            vmem((8, 128), jnp.int32),
            blocks, blocks, blocks, blocks, blocks, early_blocks, early_blocks,
            vmem((n_chunks, half, capacity, CHUNK), bf16),
            vmem((8, 128), jnp.int32),
            vmem((half, 8, 128), jnp.int32),
            vmem((most, features), bf16),
            vmem((n_kv, n_kv), bf16),
            vmem((most, n_kv), bf16),
            vmem((STEPS, own_kv, most, HD), bf16),
            vmem((STEPS, 2, own_kv, most, HD), bf16),
            vmem((kv_chunks, features, CHUNK), bf16),
            vmem((SLOTS, features, CHUNK), bf16),
            vmem((chunk_heads * rows, rows), jnp.float32),
            vmem((chunk_heads * early_rows, early_rows), jnp.float32),
            vmem((early_rows, CHUNK), jnp.float32),
            vmem((early_rows, rows), bf16),
            vmem((n_late * capacity, rows), bf16),
            vmem((2, most, CHUNK), bf16),
            vmem((n_late, capacity, width), bf16),
            vmem((half, capacity, width), bf16),
            dma((n_chunks,)), dma((n_chunks,)), dma((n_chunks,)), dma, dma,
            dma((kv_chunks,)), dma((SLOTS,)), dma((STEPS,)), dma((STEPS,)),
            dma((n_chunks,)), dma((n_chunks,)), dma((n_chunks,)), dma((n_chunks,)),
            dma((n_late,)), dma((n_late,)), dma((half + 1,)),
            dma((half, n_chunks)), dma((half, n_chunks)), dma((n_chunks,)), dma((n_chunks,)),
            dma((half,)), dma((half,)),
        ],
        compiler_params=pltpu.CompilerParams(
            collective_id=0, has_side_effects=True, vmem_limit_bytes=67043328
        ),
    )(hidden[0], doc_lengths[0], doc_target[0], norm_gain, q_weight[0], kv_weight[0])
    return result[None]


def solution(mesh):
    placed = (
        P("pipe", "dp", "tensor"),
        P("pipe", "dp", None),
        P("pipe", "dp", None),
        P("pipe", None),
        P("pipe", None, "tensor"),
        P("pipe", None, "tensor"),
    )
    run = on_device
    if mesh.shape["tensor"] == 2 and mesh.shape["dp"] in (4, 8, 16):
        sizes = (mesh.shape["dp"], mesh.shape["pipe"], mesh.shape["dp"])
        run = functools.partial(fused_device, sizes)
    return jax.shard_map(
        run, mesh=mesh, in_specs=placed, out_specs=P("pipe", "dp", "tensor"), check_vma=False
    )
```

profile of v0, /device:TPU:0, one launch (start us, length us, event | category | flops | bytes accessed | tf_op | source)
XLA Modules:
  0.0 91.7 jit_solution(1747085036677919481)
XLA Ops:
  0.0 88.6 %shard_map.64 = bf16[256,4096]{1,0:T(8,128)(2,1)} custom-call(bf16[128,4096]{1,0:T(8,128)(2,1)} %bitcast.8, s32[1,8]{1,0:T(1,128)} %bitcast.9, s32[1,8]{1,0:T(1,128)} %bitcast.10, f32[1,8192]{1,0:T(1,128)} %gain.1, bf16[8192,4096]{1,0:T(8,128)(2,1)} %bitcast.3.wq, bf16[8192,1024]{1,0:T(8,128)(2,1)} %bitcast.6), custom_call_target="tpu_custom_call" | custom-call | tf_op jit(solution)/shard_map/pallas_call | solution.py:556
  88.6 3.1 %copy.8 = bf16[1,256,4096]{2,1,0:T(8,128)(2,1)} copy(bf16[1,256,4096]{2,1,0:T(8,128)(2,1)} %bitcast.7) | data formatting | bytes 4194304
where the time goes:
time: 91.9 us; the launch traced here: 91.7 us
  Pallas kernels  88.6 us (96%)
  local copies, waits for them, and re-layouts  3.13 us (3%)
    pallas_call x1, Pallas kernels, fused_device(): pl.pallas_call(functools.partial(fused_kernel, sizes), out_shape=jax.Shap...  88.6 us
    unnamed x1, local copies, waits for them, and re-layouts  3.13 us

commit v1 on v0

--- a/solution.py
+++ b/solution.py
@@ -1,3 +1,4 @@
+import contextlib
 import functools
 
 import jax
@@ -104,6 +105,11 @@
 
 CHUNK = 256
 SLOTS = 6
+KV_ROWS = 1024
+LEAD = 5
+
+
+mark = contextlib.nullcontext
 
 
 def split_masks(n_dp):
@@ -114,7 +120,7 @@
 def fused_kernel(
     sizes, hidden, lengths, targets, gain, wq, wkv, out, meta,
     x_own, x_other, h_send, next_own, next_other, early_own, early_other, early_send,
-    meta_next, meta_early, normed, spread, kv_cols,
+    meta_next, meta_early, normed_first, normed_next, spread, kv_acc, squares, scales,
     kv_send, kv_heads, kv_weights, ring, mask, early_mask, valid, early_chooser, late_chooser,
     q_held, packed, early_out,
     sem_x, sem_xs, sem_xr, sem_ms, sem_mr, sem_kvw, sem_ring, sem_kvs, sem_kvr,
@@ -125,7 +131,8 @@
     rows, width = hidden.shape
     features = gain.shape[1]
     n_chunks = width // CHUNK
-    kv_chunks = wkv.shape[1] // CHUNK
+    n_kv = wkv.shape[1]
+    half_blocks = width // KV_ROWS
     own_kv = kv_heads.shape[2]
     chunk_heads = CHUNK // HD
     group_chunks = n_chunks // own_kv
@@ -139,8 +146,8 @@
     other = 1 - side
     following = lax.rem(pipe + 1, n_pipe)
     preceding = lax.rem(pipe + n_pipe - 1, n_pipe)
-    total = STEPS * n_chunks
-    layer_rows = (rows, rows + early_rows)
+    total = STEPS * n_chunks + LEAD
+    normed_of = (normed_first, normed_next)
 
     def partner(flips):
         index, bit = dp, 1
@@ -156,8 +163,14 @@
     def cols(j):
         return pl.ds(pl.multiple_of(j * CHUNK, CHUNK), CHUNK)
 
-    def kv_copy(n):
-        return pltpu.make_async_copy(wkv.at[:, cols(n)], kv_weights.at[n], sem_kvw.at[n])
+    def kv_rows(which, b):
+        return pl.ds(pl.multiple_of((which * half_blocks + b) * KV_ROWS, KV_ROWS), KV_ROWS)
+
+    def kv_copy(order, b):
+        here = kv_rows((side, other)[order], b)
+        return pltpu.make_async_copy(
+            wkv.at[here], kv_weights.at[here], sem_kvw.at[order * half_blocks + b]
+        )
 
     def ring_copy(c):
         slot = lax.rem(c, SLOTS)
@@ -170,7 +183,7 @@
 
     def x_remote(j):
         return pltpu.make_async_remote_copy(
-            hidden.at[:, cols(j)], x_other.at[j], sem_xs.at[j], sem_xr.at[j],
+            x_own.at[j], x_other.at[j], sem_xs.at[j], sem_xr.at[j],
             device_id={"tensor": other}, device_id_type=pl.DeviceIdType.MESH,
         )
 
@@ -199,10 +212,14 @@
             device_id={"tensor": other}, device_id_type=pl.DeviceIdType.MESH,
         )
 
-    def kv_remote(layer):
-        here = pl.ds(0, layer_rows[layer])
-        return pltpu.make_async_remote_copy(
-            kv_send.at[layer, :, here], kv_heads.at[layer, side, :, here], sem_kvs.at[layer], sem_kvr.at[layer],
+    parts = ((0, 0, rows), (1, 0, rows), (1, rows, early_rows))
+
+    def kv_remote(part):
+        layer, first, count = parts[part]
+        here = pl.ds(first, count)
+        return pltpu.make_async_remote_copy(
+            kv_send.at[layer, :, here], kv_heads.at[layer, side, :, here],
+            sem_kvs.at[part], sem_kvr.at[part],
             device_id={"tensor": other}, device_id_type=pl.DeviceIdType.MESH,
         )
 
@@ -256,14 +273,6 @@
 
     for j in range(n_chunks):
         x_copy(j).start()
-    for n in range(kv_chunks):
-        kv_copy(n).start()
-    for c in range(SLOTS):
-        ring_copy(c).start()
-
-    meta[...] = jnp.zeros(meta.shape, jnp.int32)
-    meta[0:1, 0:docs] = lengths[...]
-    meta[1:2, 0:docs] = targets[...]
     barrier = pltpu.get_barrier_semaphore()
     pl.semaphore_signal(
         barrier, inc=1, device_id={"tensor": other}, device_id_type=pl.DeviceIdType.MESH
@@ -282,12 +291,13 @@
             barrier, inc=1, device_id={"dp": lax.rem(dp + away, n_dp)},
             device_id_type=pl.DeviceIdType.MESH,
         )
-    pl.semaphore_wait(barrier, greeted)
-    for j in range(n_chunks):
-        x_remote(j).start()
-    meta_remote().start()
-
-    n_kv = kv_cols.shape[1]
+    for order in range(2):
+        for b in range(half_blocks):
+            kv_copy(order, b).start()
+
+    meta[...] = jnp.zeros(meta.shape, jnp.int32)
+    meta[0:1, 0:docs] = lengths[...]
+    meta[1:2, 0:docs] = targets[...]
     cols_wide = spread.shape[0]
     out_col = lax.broadcasted_iota(jnp.int32, (128, n_kv), 1)
     wanted = lax.rem(out_col, HD) * KV_HEADS + out_col // HD
@@ -297,8 +307,6 @@
         row = lax.broadcasted_iota(jnp.int32, (128, n_kv), 0) + base
         spread[pl.ds(base, 128), :] = (row == wanted).astype(jnp.float32).astype(jnp.bfloat16)
         return carry
-
-    lax.fori_loop(0, cols_wide // 128, fill_spread, 0)
 
     def fill_mask(source):
         row = lax.broadcasted_iota(jnp.int32, (rows, rows), 0)
@@ -348,56 +356,73 @@
             slot = lax.broadcasted_iota(jnp.int32, ref.shape, 0)
             ref[...] = (slot == goal).astype(jnp.float32).astype(jnp.bfloat16)
 
-    def normalise(mine, theirs, first, count):
-        held_rows = pl.ds(first, count)
-
-        def squares(j, acc):
-            a = mine[j].astype(jnp.float32)
-            b = theirs[j].astype(jnp.float32)
-            return acc + a * a + b * b
-
-        acc = lax.fori_loop(0, n_chunks, squares, jnp.zeros((count, CHUNK), jnp.float32))
-        scale = lax.rsqrt(jnp.sum(acc, axis=-1, keepdims=True) / features + 1e-05)
-
-        def write(j, carry):
-            for held, half in ((mine, side), (theirs, other)):
-                where = cols(half * n_chunks + j)
-                wide = held[j].astype(jnp.float32) * scale * gain[:, where]
-                normed[held_rows, where] = wide.astype(jnp.bfloat16)
+    def absorb_half(held, which):
+        def one(j, acc):
+            wide = held[j].astype(jnp.float32)
+            where = cols(which * n_chunks + j)
+            normed_first[:, where] = (wide * gain[:, where]).astype(jnp.bfloat16)
+            return acc + wide * wide
+
+        squares[0:rows] = lax.fori_loop(0, n_chunks, one, squares[0:rows])
+
+    def multiply_half(order):
+        which = (side, other)[order]
+
+        def one(b, carry):
+            kv_copy(order, b).wait()
+            here = kv_rows(which, b)
+            kv_acc[0:rows] += jnp.dot(
+                normed_first[:, here], kv_weights[here, :], preferred_element_type=jnp.float32
+            )
             return carry
 
-        lax.fori_loop(0, n_chunks, write, 0)
-
-    def keys_values(layer):
-        count = layer_rows[layer]
-
-        def one(n, carry):
-            if layer == 0:
-                kv_copy(n).wait()
-            kv_cols[0:count, cols(n)] = jnp.dot(
-                normed[0:count, :], kv_weights[n], preferred_element_type=jnp.float32
-            ).astype(jnp.bfloat16)
-            return carry
-
-        lax.fori_loop(0, kv_chunks, one, 0)
+        lax.fori_loop(0, half_blocks, one, 0)
+
+    def absorb_next(mine, theirs, first, count, j):
+        here = slice(first, first + count)
+        left, right = cols(side * n_chunks + j), cols(other * n_chunks + j)
+        a = mine[j].astype(jnp.float32)
+        b = theirs[j].astype(jnp.float32)
+        squares[here] += a * a + b * b
+        a = (a * gain[:, left]).astype(jnp.bfloat16)
+        b = (b * gain[:, right]).astype(jnp.bfloat16)
+        normed_next[here, left] = a
+        normed_next[here, right] = b
+        kv_acc[here] += jnp.dot(
+            jnp.concatenate([a, b], axis=1),
+            jnp.concatenate([kv_weights[left, :], kv_weights[right, :]], axis=0),
+            preferred_element_type=jnp.float32,
+        )
+
+    def clear_sums():
+        kv_acc[...] = jnp.zeros(kv_acc.shape, jnp.float32)
+        squares[...] = jnp.zeros(squares.shape, jnp.float32)
+
+    def keys_values(part):
+        layer, first, count = parts[part]
+        here = slice(first, first + count)
+        scale = lax.rsqrt(jnp.sum(squares[here], axis=-1, keepdims=True) / features + 1e-05)
+        scales[here] = jnp.broadcast_to(scale, (count, CHUNK))
+        kv_cols = (kv_acc[here] * scale).astype(jnp.bfloat16)
         for which, keep in ((other, False), (side, True)):
-            first = pl.multiple_of(which * own_kv * HD, own_kv * HD)
+            start = pl.multiple_of(which * own_kv * HD, own_kv * HD)
             heads = jnp.dot(
-                kv_cols[0:count, :], spread[:, pl.ds(first, own_kv * HD)],
-                preferred_element_type=jnp.float32,
+                kv_cols, spread[:, pl.ds(start, own_kv * HD)], preferred_element_type=jnp.float32
             ).astype(jnp.bfloat16)
             for g in range(own_kv):
                 if keep:
-                    kv_heads[layer, side, g, 0:count] = heads[:, g * HD:(g + 1) * HD]
+                    kv_heads[layer, side, g, here] = heads[:, g * HD:(g + 1) * HD]
                 else:
-                    kv_send[layer, g, 0:count] = heads[:, g * HD:(g + 1) * HD]
+                    kv_send[layer, g, here] = heads[:, g * HD:(g + 1) * HD]
             if not keep:
-                kv_remote(layer).start()
-
-    def query(layer, c):
-        return jnp.dot(
-            normed[0:layer_rows[layer], :], ring[lax.rem(c, SLOTS)], preferred_element_type=jnp.float32
-        ).astype(jnp.bfloat16)
+                kv_remote(part).start()
+
+    def query(layer, c, first, count):
+        here = slice(first, first + count)
+        product = jnp.dot(
+            normed_of[layer][here, :], ring[lax.rem(c, SLOTS)], preferred_element_type=jnp.float32
+        )
+        return (product * scales[here]).astype(jnp.bfloat16)
 
     def attend(layer, j, mine, first, count, allowed):
         here = slice(first, first + count)
@@ -416,39 +441,41 @@
         )
         return (mine[j].astype(jnp.float32) + side_by_side).astype(jnp.bfloat16)
 
-    def attend_all(layer, j):
-        if layer == 0:
-            return (attend(0, j, x_own, 0, rows, mask),)
-        return (
-            attend(1, j, next_own, 0, rows, mask),
-            attend(1, j, early_own, rows, early_rows, early_mask),
-        )
+    def attend_first(j):
+        return attend(0, j, x_own, 0, rows, mask)
+
+    def attend_local(j):
+        return attend(1, j, next_own, 0, rows, mask)
+
+    def attend_early(j):
+        return attend(1, j, early_own, rows, early_rows, early_mask)
 
     def refill(c):
         @pl.when(c + SLOTS < total)
         def _():
             ring_copy(c + SLOTS).start()
 
-    def run_layer(layer, finish):
-        count = layer_rows[layer]
-        base = layer * n_chunks
-        ring_copy(base).wait()
-        q_held[0, 0:count] = query(layer, base)
-        refill(jnp.int32(base))
-        kv_remote(layer).wait()
+    def run_span(layer, base, low, high, first, count, attends, finish, ready=None):
+        here = slice(first, first + count)
+        ring_copy(base + low).wait()
+        q_held[low % 2, here] = query(layer, base + low, first, count)
+        refill(jnp.int32(base + low))
+        if ready is not None:
+            ready()
 
         def one(j, carry):
             c = base + j
             ring_copy(c).wait()
-            fresh = query(layer, c)
-            done = attend_all(layer, j - 1)
-            q_held[lax.rem(j, 2), 0:count] = fresh
+            fresh = query(layer, c, first, count)
+            done = [attended(j - 1) for attended in attends]
+            q_held[lax.rem(j, 2), here] = fresh
             refill(c)
             finish(j - 1, *done)
             return carry
 
-        lax.fori_loop(1, n_chunks, one, 0)
-        finish(n_chunks - 1, *attend_all(layer, n_chunks - 1))
+        if high - low > 1:
+            lax.fori_loop(low + 1, high, one, 0)
+        finish(high - 1, *[attended(high - 1) for attended in attends])
 
     lag, early_lag = 4, 7
 
@@ -463,75 +490,129 @@
         for k in range(half):
             early_remote(k, j).start()
 
+    def take_local(j):
+        forward_remote(j).wait_recv()
+        absorb_next(next_own, next_other, 0, rows, j)
+
     def pass_early(j):
         for k in range(half):
             early_remote(k, j).wait_recv()
         early_forward(j).start()
 
+    def take_early(j):
+        early_forward(j).wait_recv()
+        absorb_next(early_own, early_other, rows, early_rows, j)
+
     def send_next(j, done):
         h_send[j] = done
         h_remote(j).start()
 
-        @pl.when(j >= lag)
-        def _():
-            pass_on(j - lag)
-
-        @pl.when(j >= early_lag)
-        def _():
-            pass_early(j - early_lag)
-
-    def send_docs(j, done, early):
+        for delay, step in (
+            (lag, pass_on), (lag + 1, take_local), (early_lag, pass_early), (early_lag + 1, take_early)
+        ):
+            @pl.when(j >= delay)
+            def _(delay=delay, step=step):
+                step(j - delay)
+
+    def send_docs(j, done):
         picked = jnp.dot(late_chooser[...], done, preferred_element_type=jnp.float32)
         picked = picked.astype(jnp.bfloat16)
-        kept = jnp.where(valid[...] > 0.0, early.astype(jnp.float32), 0.0).astype(jnp.bfloat16)
         for slot in range(len(late_masks)):
             packed[slot, :, cols(j)] = picked[slot * capacity:(slot + 1) * capacity]
         for k in reversed(range(1, len(late_masks))):
             doc_remote(k, j).start()
         own_store(j).start()
+
+    def store_early(j, early):
+        kept = jnp.where(valid[...] > 0.0, early.astype(jnp.float32), 0.0).astype(jnp.bfloat16)
         for slot in range(half):
             early_out[slot, :, cols(j)] = kept[slot * capacity:(slot + 1) * capacity]
         for slot in range(half):
             early_store(slot, j).start()
 
+    def send_and_store(j, done, early):
+        send_docs(j, done)
+        store_early(j, early)
+
+    lax.fori_loop(0, cols_wide // 128, fill_spread, 0)
     fill_mask(meta)
     fill_early_mask()
-    meta_remote().wait()
-    for k in range(half):
-        meta_on(k).start()
-    fill_choosers(meta_next)
-    for j in range(n_chunks):
-        x_copy(j).wait()
-    for j in range(n_chunks):
-        x_remote(j).wait()
-    normalise(x_own, x_other, 0, rows)
-    keys_values(0)
-    run_layer(0, send_next)
-    for j in range(n_chunks - lag, n_chunks):
-        pass_on(j)
-    fill_mask(meta_next)
-    for k in range(half):
-        meta_on(k).wait()
-    fill_valid()
-    for j in range(n_chunks - early_lag, n_chunks):
-        pass_early(j)
-    for j in range(n_chunks):
-        forward_remote(j).wait()
-    normalise(next_own, next_other, 0, rows)
-    for j in range(n_chunks):
-        early_forward(j).wait()
-    normalise(early_own, early_other, rows, early_rows)
-    keys_values(1)
-    run_layer(1, send_docs)
-    for j in range(n_chunks):
-        h_remote(j).wait_send()
+    clear_sums()
+    with mark("PX_barrier"):
+        pl.semaphore_wait(barrier, greeted)
+    with mark("P1_xsend"):
+        for j in range(n_chunks):
+            x_copy(j).wait()
+            x_remote(j).start()
+    meta_remote().start()
+    for c in range(SLOTS):
+        ring_copy(c).start()
+    with mark("P2_own"):
+        absorb_half(x_own, side)
+        multiply_half(0)
+    with mark("P3_xwait"):
+        for j in range(n_chunks):
+            x_remote(j).wait()
+    with mark("P4_other"):
+        absorb_half(x_other, other)
+        multiply_half(1)
+    with mark("P5_kv"):
+        keys_values(0)
+        clear_sums()
+    with mark("P6_first"):
+        run_span(0, 0, 0, 1, 0, rows, (attend_first,), send_next, kv_remote(0).wait)
+    with mark("P7_meta"):
+        meta_remote().wait()
         for k in range(half):
-            early_remote(k, j).wait_send()
-    for slot in range(half):
-        early_stored(slot).wait()
-    own_stored().wait()
-    for k in range(1, len(late_masks)):
-        doc_all(k).wait()
+            meta_on(k).start()
+        fill_choosers(meta_next)
+    with mark("P8_layer0"):
+        run_span(0, 0, 1, n_chunks, 0, rows, (attend_first,), send_next)
+    with mark("P9_rest"):
+        fill_mask(meta_next)
+        for k in range(half):
+            meta_on(k).wait()
+        fill_valid()
+        behind = early_lag - lag
+        for j in range(n_chunks - lag, n_chunks):
+            pass_on(j)
+            take_local(j - 1)
+            pass_early(j - behind)
+            take_early(j - 1 - behind)
+    with mark("PA_last"):
+        take_local(n_chunks - 1)
+    with mark("PB_kv"):
+        keys_values(1)
+    with mark("PC_first"):
+        run_span(1, n_chunks, 0, 1, 0, rows, (attend_local,), send_docs, kv_remote(1).wait)
+    with mark("PD_local"):
+        run_span(1, n_chunks, 1, LEAD, 0, rows, (attend_local,), send_docs)
+    with mark("PE_early"):
+        for j in range(n_chunks - behind, n_chunks):
+            pass_early(j)
+            take_early(j - 1)
+        take_early(n_chunks - 1)
+        keys_values(2)
+    with mark("PF_both"):
+        run_span(
+            1, n_chunks, LEAD, n_chunks, 0, rows + early_rows, (attend_local, attend_early),
+            send_and_store, kv_remote(2).wait,
+        )
+    with mark("PG_early"):
+        run_span(1, STEPS * n_chunks, 0, LEAD, rows, early_rows, (attend_early,), store_early)
+    with mark("PH_sends"):
+        for j in range(n_chunks):
+            h_remote(j).wait_send()
+            forward_remote(j).wait_send()
+            early_forward(j).wait_send()
+            for k in range(half):
+                early_remote(k, j).wait_send()
+        for slot in range(half):
+            early_stored(slot).wait()
+        own_stored().wait()
+    with mark("PI_docs"):
+        for k in range(1, len(late_masks)):
+            doc_all(k).wait()
 
 
 def fused_device(sizes, hidden, doc_lengths, doc_target, norm_gain, q_weight, kv_weight):
@@ -540,7 +621,6 @@
     features = norm_gain.shape[1]
     n_chunks = width // CHUNK
     n_kv = kv_weight.shape[2]
-    kv_chunks = n_kv // CHUNK
     own_kv = KV_HEADS // 2
     capacity = rows // 4
     chunk_heads = CHUNK // HD
@@ -571,12 +651,15 @@
             vmem((n_chunks, half, capacity, CHUNK), bf16),
             vmem((8, 128), jnp.int32),
             vmem((half, 8, 128), jnp.int32),
+            vmem((rows, features), bf16),
             vmem((most, features), bf16),
             vmem((n_kv, n_kv), bf16),
-            vmem((most, n_kv), bf16),
+            vmem((most, n_kv), jnp.float32),
+            vmem((most, CHUNK), jnp.float32),
+            vmem((most, CHUNK), jnp.float32),
             vmem((STEPS, own_kv, most, HD), bf16),
             vmem((STEPS, 2, own_kv, most, HD), bf16),
-            vmem((kv_chunks, features, CHUNK), bf16),
+            vmem((features, n_kv), bf16),
             vmem((SLOTS, features, CHUNK), bf16),
             vmem((chunk_heads * rows, rows), jnp.float32),
             vmem((chunk_heads * early_rows, early_rows), jnp.float32),
@@ -587,7 +670,7 @@
             vmem((n_late, capacity, width), bf16),
             vmem((half, capacity, width), bf16),
             dma((n_chunks,)), dma((n_chunks,)), dma((n_chunks,)), dma, dma,
-            dma((kv_chunks,)), dma((SLOTS,)), dma((STEPS,)), dma((STEPS,)),
+            dma((features // KV_ROWS,)), dma((SLOTS,)), dma((STEPS + 1,)), dma((STEPS + 1,)),
             dma((n_chunks,)), dma((n_chunks,)), dma((n_chunks,)), dma((n_chunks,)),
             dma((n_late,)), dma((n_late,)), dma((half + 1,)),
             dma((half, n_chunks)), dma((half, n_chunks)), dma((n_chunks,)), dma((n_chunks,)),

time: 91.9 us -> 80.6 us (0.88)
  Pallas kernels: 88.6 us -> 77.3 us
    pallas_call x1, Pallas kernels: 88.6 us -> 77.3 us  [fused_device(): pl.pallas_call(functools.partial(fused_kernel, sizes), out_shape=jax.Shap...]
where the time goes in v1:
time: 80.6 us; the launch traced here: 80.4 us
  Pallas kernels  77.3 us (96%)
  local copies, waits for them, and re-layouts  3.13 us (4%)
    pallas_call x1, Pallas kernels, fused_device(): pl.pallas_call(functools.partial(fused_kernel, sizes), out_shape=jax.Shap...  77.3 us
    unnamed x1, local copies, waits for them, and re-layouts  3.13 us

profile of v1, /device:TPU:0, one launch (start us, length us, event | category | flops | bytes accessed | tf_op | source)
XLA Modules:
  0.0 80.4 jit_solution(11939702729499005866)
XLA Ops:
  0.0 77.3 %shard_map.64 = bf16[256,4096]{1,0:T(8,128)(2,1)} custom-call(bf16[128,4096]{1,0:T(8,128)(2,1)} %bitcast.8, s32[1,8]{1,0:T(1,128)} %bitcast.9, s32[1,8]{1,0:T(1,128)} %bitcast.10, f32[1,8192]{1,0:T(1,128)} %gain.1, bf16[8192,4096]{1,0:T(8,128)(2,1)} %bitcast.3.wq, bf16[8192,1024]{1,0:T(8,128)(2,1)} %bitcast.6), custom_call_target="tpu_custom_call" | custom-call | tf_op jit(solution)/shard_map/pallas_call | solution.py:636
  77.3 3.1 %copy.8 = bf16[1,256,4096]{2,1,0:T(8,128)(2,1)} copy(bf16[1,256,4096]{2,1,0:T(8,128)(2,1)} %bitcast.7) | data formatting | bytes 4194304

commit v2 on v1

--- a/solution.py
+++ b/solution.py
@@ -106,7 +106,8 @@
 CHUNK = 256
 SLOTS = 6
 KV_ROWS = 1024
-LEAD = 5
+LEAD = 4
+PIECES = 4
 
 
 mark = contextlib.nullcontext
@@ -417,12 +418,12 @@
             if not keep:
                 kv_remote(part).start()
 
-    def query(layer, c, first, count):
-        here = slice(first, first + count)
-        product = jnp.dot(
-            normed_of[layer][here, :], ring[lax.rem(c, SLOTS)], preferred_element_type=jnp.float32
-        )
-        return (product * scales[here]).astype(jnp.bfloat16)
+    def query_piece(layer, c, first, count, piece):
+        deep = slice(piece * features // PIECES, (piece + 1) * features // PIECES)
+        return jnp.dot(
+            normed_of[layer][first:first + count, deep], ring[lax.rem(c, SLOTS), deep],
+            preferred_element_type=jnp.float32,
+        )
 
     def attend(layer, j, mine, first, count, allowed):
         here = slice(first, first + count)
@@ -433,13 +434,15 @@
             stacked, kv_heads[layer, 0, g, here], (((1,), (1,)), ((), ())),
             preferred_element_type=jnp.float32,
         ) * HD ** (-0.5)
+        yield
         e = jnp.where(allowed[...] > 0.0, jnp.exp(scores), 0.0)
         p = (e * (1.0 / jnp.sum(e, axis=-1, keepdims=True))).astype(jnp.bfloat16)
+        yield
         a = jnp.dot(p, kv_heads[layer, 1, g, here], preferred_element_type=jnp.float32)
         side_by_side = jnp.concatenate(
             [a[i * count:(i + 1) * count] for i in range(chunk_heads)], axis=1
         )
-        return (mine[j].astype(jnp.float32) + side_by_side).astype(jnp.bfloat16)
+        yield (mine[j].astype(jnp.float32) + side_by_side).astype(jnp.bfloat16)
 
     def attend_first(j):
         return attend(0, j, x_own, 0, rows, mask)
@@ -455,84 +458,123 @@
         def _():
             ring_copy(c + SLOTS).start()
 
-    def run_span(layer, base, low, high, first, count, attends, finish, ready=None):
+    def first_query(layer, c, first, count):
+        ring_copy(c).wait()
+        product = query_piece(layer, c, first, count, 0)
+        for piece in range(1, PIECES):
+            product = product + query_piece(layer, c, first, count, piece)
+        q_held[0, first:first + count] = (product * scales[first:first + count]).astype(jnp.bfloat16)
+        refill(jnp.int32(c))
+
+    def step(layer, c, slot, first, count, before, attends, settles, extras=()):
+        ring_copy(c).wait()
+        stages = [attended(before) for attended in attends]
+        product = None
+        for piece in range(PIECES):
+            done = [next(stage, None) for stage in stages]
+            if piece == 2:
+                made = done
+            if piece == 3:
+                for settle, value in zip(settles, made):
+                    settle(before, value)
+            for extra in extras[piece:piece + 1]:
+                extra()
+            part = query_piece(layer, c, first, count, piece)
+            product = part if product is None else product + part
         here = slice(first, first + count)
-        ring_copy(base + low).wait()
-        q_held[low % 2, here] = query(layer, base + low, first, count)
-        refill(jnp.int32(base + low))
-        if ready is not None:
-            ready()
-
-        def one(j, carry):
-            c = base + j
-            ring_copy(c).wait()
-            fresh = query(layer, c, first, count)
-            done = [attended(j - 1) for attended in attends]
-            q_held[lax.rem(j, 2), here] = fresh
-            refill(c)
-            finish(j - 1, *done)
-            return carry
-
-        if high - low > 1:
-            lax.fori_loop(low + 1, high, one, 0)
-        finish(high - 1, *[attended(high - 1) for attended in attends])
-
-    lag, early_lag = 4, 7
-
-    def pass_on(j):
+        q_held[slot, here] = (product * scales[here]).astype(jnp.bfloat16)
+
+    def last_step(before, attends, settles):
+        stages = [attended(before) for attended in attends]
+        for piece in range(3):
+            made = [next(stage) for stage in stages]
+        for settle, value in zip(settles, made):
+            settle(before, value)
+
+    def keep_next(j, done):
+        h_send[j] = done
+
+    def pass_on_start(j):
         h_remote(j).wait_recv()
         forward_remote(j).start()
+
+    def pass_on_pick(j):
         picked = jnp.dot(
             early_chooser[...], next_own[j], preferred_element_type=jnp.float32
         ).astype(jnp.bfloat16)
         for slot in range(half):
             early_send[j, slot] = picked[slot * capacity:(slot + 1) * capacity]
+
+    def pass_on_send(j):
         for k in range(half):
             early_remote(k, j).start()
 
-    def take_local(j):
-        forward_remote(j).wait_recv()
+    def pass_on(j):
+        pass_on_start(j)
+        pass_on_pick(j)
+        pass_on_send(j)
+
+    def absorb_local(j):
         absorb_next(next_own, next_other, 0, rows, j)
+
+    def absorb_early(j):
+        absorb_next(early_own, early_other, rows, early_rows, j)
 
     def pass_early(j):
         for k in range(half):
             early_remote(k, j).wait_recv()
         early_forward(j).start()
 
-    def take_early(j):
-        early_forward(j).wait_recv()
-        absorb_next(early_own, early_other, rows, early_rows, j)
-
-    def send_next(j, done):
-        h_send[j] = done
-        h_remote(j).start()
-
-        for delay, step in (
-            (lag, pass_on), (lag + 1, take_local), (early_lag, pass_early), (early_lag + 1, take_early)
-        ):
-            @pl.when(j >= delay)
-            def _(delay=delay, step=step):
-                step(j - delay)
-
-    def send_docs(j, done):
+    def pick_docs(j, done):
         picked = jnp.dot(late_chooser[...], done, preferred_element_type=jnp.float32)
         picked = picked.astype(jnp.bfloat16)
         for slot in range(len(late_masks)):
             packed[slot, :, cols(j)] = picked[slot * capacity:(slot + 1) * capacity]
+
+    def send_docs(j):
         for k in reversed(range(1, len(late_masks))):
             doc_remote(k, j).start()
         own_store(j).start()
 
-    def store_early(j, early):
+    def keep_early(j, early):
         kept = jnp.where(valid[...] > 0.0, early.astype(jnp.float32), 0.0).astype(jnp.bfloat16)
         for slot in range(half):
             early_out[slot, :, cols(j)] = kept[slot * capacity:(slot + 1) * capacity]
+
+    def store_early(j):
         for slot in range(half):
             early_store(slot, j).start()
 
-    def send_and_store(j, done, early):
-        send_docs(j, done)
-        store_early(j, early)
+    lag, early_lag = 5, 10
+
+    def first_span(low, high, stage):
+        def one(j, carry):
+            on, local, gone, early = j - lag, j - lag - 1, j - early_lag, j - early_lag - 1
+            extras = [[], [], [], []]
+            if stage >= 1:
+                pass_on_start(on)
+                forward_remote(local).wait_recv()
+                extras[0].append(functools.partial(absorb_local, local))
+                extras[1].append(functools.partial(pass_on_pick, on))
+            if stage >= 2:
+                pass_early(gone)
+                early_forward(early).wait_recv()
+                extras[2].append(functools.partial(absorb_early, early))
+            step(
+                0, j, lax.rem(j, 2), 0, rows, j - 1, (attend_first,), (keep_next,),
+                [functools.partial(run_all, group) for group in extras],
+            )
+            h_remote(j - 1).start()
+            if stage >= 1:
+                pass_on_send(on)
+            refill(j)
+            return carry
+
+        lax.fori_loop(low, high, one, 0)
+
+    def run_all(group):
+        for task in group:
+            task()
 
     lax.fori_loop(0, cols_wide // 128, fill_spread, 0)
     fill_mask(meta)
@@ -560,47 +602,105 @@
         keys_values(0)
         clear_sums()
     with mark("P6_first"):
-        run_span(0, 0, 0, 1, 0, rows, (attend_first,), send_next, kv_remote(0).wait)
-    with mark("P7_meta"):
+        first_query(0, 0, 0, rows)
+        kv_remote(0).wait()
+    with mark("P7_span0"):
+        first_span(1, lag + 1, 0)
+    with mark("P8_meta"):
         meta_remote().wait()
         for k in range(half):
             meta_on(k).start()
         fill_choosers(meta_next)
-    with mark("P8_layer0"):
-        run_span(0, 0, 1, n_chunks, 0, rows, (attend_first,), send_next)
-    with mark("P9_rest"):
+        pass_on(0)
+    with mark("P9_span1"):
+        first_span(lag + 1, early_lag + 1, 1)
+    with mark("PA_early0"):
+        pass_early(0)
+    with mark("PB_span2"):
+        first_span(early_lag + 1, n_chunks, 2)
+    with mark("PC_rest"):
+        last_step(n_chunks - 1, (attend_first,), (keep_next,))
+        h_remote(n_chunks - 1).start()
         fill_mask(meta_next)
         for k in range(half):
             meta_on(k).wait()
         fill_valid()
-        behind = early_lag - lag
+        gone = n_chunks - early_lag
         for j in range(n_chunks - lag, n_chunks):
-            pass_on(j)
-            take_local(j - 1)
-            pass_early(j - behind)
-            take_early(j - 1 - behind)
-    with mark("PA_last"):
-        take_local(n_chunks - 1)
-    with mark("PB_kv"):
+            pass_on_start(j)
+            pass_on_pick(j)
+            pass_on_send(j)
+            forward_remote(j - 1).wait_recv()
+            absorb_local(j - 1)
+            for _ in range(2):
+                if gone < j - 3:
+                    pass_early(gone)
+                    early_forward(gone - 1).wait_recv()
+                    absorb_early(gone - 1)
+                    gone += 1
+    with mark("PD_last"):
+        forward_remote(n_chunks - 1).wait_recv()
+        absorb_local(n_chunks - 1)
+    with mark("PE_kv"):
         keys_values(1)
-    with mark("PC_first"):
-        run_span(1, n_chunks, 0, 1, 0, rows, (attend_local,), send_docs, kv_remote(1).wait)
-    with mark("PD_local"):
-        run_span(1, n_chunks, 1, LEAD, 0, rows, (attend_local,), send_docs)
-    with mark("PE_early"):
-        for j in range(n_chunks - behind, n_chunks):
-            pass_early(j)
-            take_early(j - 1)
-        take_early(n_chunks - 1)
-        keys_values(2)
-    with mark("PF_both"):
-        run_span(
-            1, n_chunks, LEAD, n_chunks, 0, rows + early_rows, (attend_local, attend_early),
-            send_and_store, kv_remote(2).wait,
-        )
-    with mark("PG_early"):
-        run_span(1, STEPS * n_chunks, 0, LEAD, rows, early_rows, (attend_early,), store_early)
-    with mark("PH_sends"):
+    with mark("PF_first"):
+        first_query(1, n_chunks, 0, rows)
+        kv_remote(1).wait()
+    with mark("PG_local"):
+        ready = gone - 1
+        for j in range(1, LEAD + 1):
+            count = rows + early_rows if j == LEAD else rows
+            waiting = [] if j == 1 else [i for i in range(ready, ready + j - 1) if j < LEAD]
+            for i in waiting:
+                early_forward(i).wait_recv()
+            ready += len(waiting)
+            step(
+                1, n_chunks + j, j % 2, 0, count, j - 1, (attend_local,), (pick_docs,),
+                [functools.partial(absorb_early, i) for i in waiting],
+            )
+            send_docs(j - 1)
+            refill(jnp.int32(n_chunks + j))
+            if j == 1:
+                for i in range(gone, n_chunks):
+                    pass_early(i)
+            if j == LEAD - 1:
+                for i in range(ready, n_chunks):
+                    early_forward(i).wait_recv()
+                    absorb_early(i)
+                keys_values(2)
+        kv_remote(2).wait()
+    with mark("PH_both"):
+        def both(j, carry):
+            step(
+                1, n_chunks + j, lax.rem(j, 2), 0, rows + early_rows, j - 1,
+                (attend_local, attend_early), (pick_docs, keep_early),
+            )
+            send_docs(j - 1)
+            store_early(j - 1)
+            refill(n_chunks + j)
+            return carry
+
+        lax.fori_loop(LEAD + 1, n_chunks, both, 0)
+    with mark("PI_turn"):
+        step(
+            1, total - LEAD, 0, rows, early_rows, n_chunks - 1,
+            (attend_local, attend_early), (pick_docs, keep_early),
+        )
+        send_docs(n_chunks - 1)
+        store_early(n_chunks - 1)
+    with mark("PJ_early"):
+        def behind(j, carry):
+            step(
+                1, total - LEAD + j, lax.rem(j, 2), rows, early_rows, j - 1,
+                (attend_early,), (keep_early,),
+            )
+            store_early(j - 1)
+            return carry
+
+        lax.fori_loop(1, LEAD, behind, 0)
+        last_step(LEAD - 1, (attend_early,), (keep_early,))
+        store_early(LEAD - 1)
+    with mark("PK_sends"):
         for j in range(n_chunks):
             h_remote(j).wait_send()
             forward_remote(j).wait_send()
@@ -610,7 +710,7 @@
         for slot in range(half):
             early_stored(slot).wait()
         own_stored().wait()
-    with mark("PI_docs"):
+    with mark("PL_docs"):
         for k in range(1, len(late_masks)):
             doc_all(k).wait()
 

time: 80.6 us -> 76.5 us (0.949)
  Pallas kernels: 77.3 us -> 73.1 us
    pallas_call x1, Pallas kernels: 77.3 us -> 73.1 us  [fused_device(): pl.pallas_call(functools.partial(fused_kernel, sizes), out_shape=jax.Shap...]
where the time goes in v2:
time: 76.5 us; the launch traced here: 76.3 us
  Pallas kernels  73.1 us (96%)
  local copies, waits for them, and re-layouts  3.13 us (4%)
    pallas_call x1, Pallas kernels, fused_device(): pl.pallas_call(functools.partial(fused_kernel, sizes), out_shape=jax.Shap...  73.1 us
    unnamed x1, local copies, waits for them, and re-layouts  3.13 us

profile of v2, /device:TPU:0, one launch (start us, length us, event | category | flops | bytes accessed | tf_op | source)
XLA Modules:
  0.0 76.3 jit_solution(9560811550335465373)
XLA Ops:
  0.0 73.1 %shard_map.64 = bf16[256,4096]{1,0:T(8,128)(2,1)} custom-call(bf16[128,4096]{1,0:T(8,128)(2,1)} %bitcast.8, s32[1,8]{1,0:T(1,128)} %bitcast.9, s32[1,8]{1,0:T(1,128)} %bitcast.10, f32[1,8192]{1,0:T(1,128)} %gain.1, bf16[8192,4096]{1,0:T(8,128)(2,1)} %bitcast.3.wq, bf16[8192,1024]{1,0:T(8,128)(2,1)} %bitcast.6), custom_call_target="tpu_custom_call" | custom-call | tf_op jit(solution)/shard_map/pallas_call | solution.py:736
  73.2 3.1 %copy.8 = bf16[1,256,4096]{2,1,0:T(8,128)(2,1)} copy(bf16[1,256,4096]{2,1,0:T(8,128)(2,1)} %bitcast.7) | data formatting | bytes 4194304

commit v3 on v2

--- a/solution.py
+++ b/solution.py
@@ -106,7 +106,7 @@
 CHUNK = 256
 SLOTS = 6
 KV_ROWS = 1024
-LEAD = 4
+LEAD = 6
 PIECES = 4
 
 
@@ -119,18 +119,18 @@
 
 
 def fused_kernel(
-    sizes, hidden, lengths, targets, gain, wq, wkv, out, meta,
+    sizes, hidden, lengths_in, targets_in, gain_in, wq, wkv, out, meta, lengths, targets, gain,
     x_own, x_other, h_send, next_own, next_other, early_own, early_other, early_send,
-    meta_next, meta_early, normed_first, normed_next, spread, kv_acc, squares, scales,
+    meta_next, meta_early, normed_first, normed_next, spread, kv_acc, kv_cols, squares, scales,
     kv_send, kv_heads, kv_weights, ring, mask, early_mask, valid, early_chooser, late_chooser,
-    q_held, packed, early_out,
+    q_held, begun, packed,
     sem_x, sem_xs, sem_xr, sem_ms, sem_mr, sem_kvw, sem_ring, sem_kvs, sem_kvr,
-    sem_hs, sem_hr, sem_fs, sem_fr, sem_as, sem_ar, sem_own,
-    sem_es, sem_er, sem_gs, sem_gr, sem_mes, sem_mer,
+    sem_hs, sem_hr, sem_fs, sem_fr, sem_as, sem_ar,
+    sem_es, sem_er, sem_gs, sem_gr, sem_mes, sem_mer, sem_in,
 ):
     n_dp, n_pipe, docs = sizes
     rows, width = hidden.shape
-    features = gain.shape[1]
+    features = gain_in.shape[1]
     n_chunks = width // CHUNK
     n_kv = wkv.shape[1]
     half_blocks = width // KV_ROWS
@@ -253,27 +253,14 @@
             device_id={"dp": late_partners[k]}, device_id_type=pl.DeviceIdType.MESH,
         )
 
-    def own_store(j):
-        return pltpu.make_async_copy(
-            packed.at[0, :, cols(j)], out.at[doc_rows(dp), cols(j)], sem_own.at[half]
-        )
-
-    def own_stored():
-        return pltpu.make_async_copy(packed.at[0], out.at[doc_rows(dp)], sem_own.at[half])
-
-    def early_store(k, j):
-        return pltpu.make_async_copy(
-            early_out.at[k, :, cols(j)], out.at[doc_rows(early_partners[k]), cols(j)],
-            sem_own.at[k],
-        )
-
-    def early_stored(k):
-        return pltpu.make_async_copy(
-            early_out.at[k], out.at[doc_rows(early_partners[k])], sem_own.at[k]
-        )
-
+    small = [
+        pltpu.make_async_copy(*pair, sem_in.at[i])
+        for i, pair in enumerate(((lengths_in, lengths), (targets_in, targets), (gain_in, gain)))
+    ]
     for j in range(n_chunks):
         x_copy(j).start()
+    for copy in small:
+        copy.start()
     barrier = pltpu.get_barrier_semaphore()
     pl.semaphore_signal(
         barrier, inc=1, device_id={"tensor": other}, device_id_type=pl.DeviceIdType.MESH
@@ -296,9 +283,6 @@
         for b in range(half_blocks):
             kv_copy(order, b).start()
 
-    meta[...] = jnp.zeros(meta.shape, jnp.int32)
-    meta[0:1, 0:docs] = lengths[...]
-    meta[1:2, 0:docs] = targets[...]
     cols_wide = spread.shape[0]
     out_col = lax.broadcasted_iota(jnp.int32, (128, n_kv), 1)
     wanted = lax.rem(out_col, HD) * KV_HEADS + out_col // HD
@@ -379,19 +363,22 @@
 
         lax.fori_loop(0, half_blocks, one, 0)
 
-    def absorb_next(mine, theirs, first, count, j):
+    def absorb_next(mine, theirs, first, count, chunks):
         here = slice(first, first + count)
-        left, right = cols(side * n_chunks + j), cols(other * n_chunks + j)
-        a = mine[j].astype(jnp.float32)
-        b = theirs[j].astype(jnp.float32)
-        squares[here] += a * a + b * b
-        a = (a * gain[:, left]).astype(jnp.bfloat16)
-        b = (b * gain[:, right]).astype(jnp.bfloat16)
-        normed_next[here, left] = a
-        normed_next[here, right] = b
+        total = squares[here]
+        left, right = [], []
+        for j in chunks:
+            for held, which in ((mine, side), (theirs, other)):
+                where = cols(which * n_chunks + j)
+                wide = held[j].astype(jnp.float32)
+                total = total + wide * wide
+                scaled = (wide * gain[:, where]).astype(jnp.bfloat16)
+                normed_next[here, where] = scaled
+                left.append(scaled)
+                right.append(kv_weights[where, :])
+        squares[here] = total
         kv_acc[here] += jnp.dot(
-            jnp.concatenate([a, b], axis=1),
-            jnp.concatenate([kv_weights[left, :], kv_weights[right, :]], axis=0),
+            jnp.concatenate(left, axis=1), jnp.concatenate(right, axis=0),
             preferred_element_type=jnp.float32,
         )
 
@@ -404,19 +391,25 @@
         here = slice(first, first + count)
         scale = lax.rsqrt(jnp.sum(squares[here], axis=-1, keepdims=True) / features + 1e-05)
         scales[here] = jnp.broadcast_to(scale, (count, CHUNK))
-        kv_cols = (kv_acc[here] * scale).astype(jnp.bfloat16)
-        for which, keep in ((other, False), (side, True)):
-            start = pl.multiple_of(which * own_kv * HD, own_kv * HD)
-            heads = jnp.dot(
-                kv_cols, spread[:, pl.ds(start, own_kv * HD)], preferred_element_type=jnp.float32
-            ).astype(jnp.bfloat16)
-            for g in range(own_kv):
-                if keep:
-                    kv_heads[layer, side, g, here] = heads[:, g * HD:(g + 1) * HD]
-                else:
-                    kv_send[layer, g, here] = heads[:, g * HD:(g + 1) * HD]
-            if not keep:
-                kv_remote(part).start()
+        kv_cols[here] = (kv_acc[here] * scale).astype(jnp.bfloat16)
+        heads = kv_spread(part, other)
+        for g in range(own_kv):
+            kv_send[layer, g, here] = heads[:, g * HD:(g + 1) * HD]
+        kv_remote(part).start()
+
+    def kv_spread(part, which):
+        _, first, count = parts[part]
+        start = pl.multiple_of(which * own_kv * HD, own_kv * HD)
+        return jnp.dot(
+            kv_cols[first:first + count], spread[:, pl.ds(start, own_kv * HD)],
+            preferred_element_type=jnp.float32,
+        ).astype(jnp.bfloat16)
+
+    def keep_heads(part):
+        layer, first, count = parts[part]
+        heads = kv_spread(part, side)
+        for g in range(own_kv):
+            kv_heads[layer, side, g, first:first + count] = heads[:, g * HD:(g + 1) * HD]
 
     def query_piece(layer, c, first, count, piece):
         deep = slice(piece * features // PIECES, (piece + 1) * features // PIECES)
@@ -458,12 +451,35 @@
         def _():
             ring_copy(c + SLOTS).start()
 
-    def first_query(layer, c, first, count):
+    def first_query(layer, c):
         ring_copy(c).wait()
-        product = query_piece(layer, c, first, count, 0)
+        product = query_piece(layer, c, 0, rows, 0)
         for piece in range(1, PIECES):
-            product = product + query_piece(layer, c, first, count, piece)
-        q_held[0, first:first + count] = (product * scales[first:first + count]).astype(jnp.bfloat16)
+            product = product + query_piece(layer, c, 0, rows, piece)
+        q_held[0, 0:rows] = (product * scales[0:rows]).astype(jnp.bfloat16)
+        refill(jnp.int32(c))
+
+    lag, early_lag = 5, 10
+    early_deep = (n_chunks - lag + 1) * CHUNK
+
+    def query_part(c, low, high):
+        product = None
+        for start in (0, width):
+            deep = slice(start + low, start + high)
+            part = jnp.dot(
+                normed_next[0:rows, deep], ring[lax.rem(c, SLOTS), deep],
+                preferred_element_type=jnp.float32,
+            )
+            product = part if product is None else product + part
+        return product
+
+    def begin_query(c):
+        ring_copy(c).wait()
+        begun[...] = query_part(c, 0, early_deep)
+
+    def end_query(c):
+        product = begun[...] + query_part(c, early_deep, width)
+        q_held[0, 0:rows] = (product * scales[0:rows]).astype(jnp.bfloat16)
         refill(jnp.int32(c))
 
     def step(layer, c, slot, first, count, before, attends, settles, extras=()):
@@ -514,11 +530,11 @@
         pass_on_pick(j)
         pass_on_send(j)
 
-    def absorb_local(j):
-        absorb_next(next_own, next_other, 0, rows, j)
-
-    def absorb_early(j):
-        absorb_next(early_own, early_other, rows, early_rows, j)
+    def absorb_local(*chunks):
+        absorb_next(next_own, next_other, 0, rows, chunks)
+
+    def absorb_early(*chunks):
+        absorb_next(early_own, early_other, rows, early_rows, chunks)
 
     def pass_early(j):
         for k in range(half):
@@ -528,24 +544,18 @@
     def pick_docs(j, done):
         picked = jnp.dot(late_chooser[...], done, preferred_element_type=jnp.float32)
         picked = picked.astype(jnp.bfloat16)
-        for slot in range(len(late_masks)):
+        out[doc_rows(dp), cols(j)] = picked[0:capacity]
+        for slot in range(1, len(late_masks)):
             packed[slot, :, cols(j)] = picked[slot * capacity:(slot + 1) * capacity]
 
     def send_docs(j):
         for k in reversed(range(1, len(late_masks))):
             doc_remote(k, j).start()
-        own_store(j).start()
 
     def keep_early(j, early):
         kept = jnp.where(valid[...] > 0.0, early.astype(jnp.float32), 0.0).astype(jnp.bfloat16)
         for slot in range(half):
-            early_out[slot, :, cols(j)] = kept[slot * capacity:(slot + 1) * capacity]
-
-    def store_early(j):
-        for slot in range(half):
-            early_store(slot, j).start()
-
-    lag, early_lag = 5, 10
+            out[doc_rows(early_partners[slot]), cols(j)] = kept[slot * capacity:(slot + 1) * capacity]
 
     def first_span(low, high, stage):
         def one(j, carry):
@@ -577,9 +587,14 @@
             task()
 
     lax.fori_loop(0, cols_wide // 128, fill_spread, 0)
-    fill_mask(meta)
     fill_early_mask()
     clear_sums()
+    for copy in small:
+        copy.wait()
+    meta[...] = jnp.zeros(meta.shape, jnp.int32)
+    meta[0:1, 0:docs] = lengths[...]
+    meta[1:2, 0:docs] = targets[...]
+    fill_mask(meta)
     with mark("PX_barrier"):
         pl.semaphore_wait(barrier, greeted)
     with mark("P1_xsend"):
@@ -600,9 +615,9 @@
         multiply_half(1)
     with mark("P5_kv"):
         keys_values(0)
-        clear_sums()
     with mark("P6_first"):
-        first_query(0, 0, 0, rows)
+        first_query(0, 0)
+        keep_heads(0)
         kv_remote(0).wait()
     with mark("P7_span0"):
         first_span(1, lag + 1, 0)
@@ -611,6 +626,7 @@
         for k in range(half):
             meta_on(k).start()
         fill_choosers(meta_next)
+        clear_sums()
         pass_on(0)
     with mark("P9_span1"):
         first_span(lag + 1, early_lag + 1, 1)
@@ -632,8 +648,10 @@
             pass_on_send(j)
             forward_remote(j - 1).wait_recv()
             absorb_local(j - 1)
+            if j == n_chunks - lag + 1:
+                begin_query(n_chunks)
             for _ in range(2):
-                if gone < j - 3:
+                if gone < j - 4:
                     pass_early(gone)
                     early_forward(gone - 1).wait_recv()
                     absorb_early(gone - 1)
@@ -644,30 +662,32 @@
     with mark("PE_kv"):
         keys_values(1)
     with mark("PF_first"):
-        first_query(1, n_chunks, 0, rows)
+        end_query(n_chunks)
+        keep_heads(1)
         kv_remote(1).wait()
     with mark("PG_local"):
-        ready = gone - 1
-        for j in range(1, LEAD + 1):
-            count = rows + early_rows if j == LEAD else rows
-            waiting = [] if j == 1 else [i for i in range(ready, ready + j - 1) if j < LEAD]
-            for i in waiting:
-                early_forward(i).wait_recv()
-            ready += len(waiting)
+        def local(j, carry):
             step(
-                1, n_chunks + j, j % 2, 0, count, j - 1, (attend_local,), (pick_docs,),
-                [functools.partial(absorb_early, i) for i in waiting],
+                1, n_chunks + j, lax.rem(j, 2), 0, rows, j - 1, (attend_local,), (pick_docs,)
             )
             send_docs(j - 1)
-            refill(jnp.int32(n_chunks + j))
-            if j == 1:
-                for i in range(gone, n_chunks):
-                    pass_early(i)
-            if j == LEAD - 1:
-                for i in range(ready, n_chunks):
-                    early_forward(i).wait_recv()
-                    absorb_early(i)
-                keys_values(2)
+            refill(n_chunks + j)
+            return carry
+
+        lax.fori_loop(1, LEAD - 1, local, 0)
+        for i in range(gone, n_chunks):
+            pass_early(i)
+        lax.fori_loop(LEAD - 1, LEAD, local, 0)
+        for i in range(gone - 1, n_chunks):
+            early_forward(i).wait_recv()
+        absorb_early(*range(gone - 1, n_chunks))
+        keys_values(2)
+        step(
+            1, n_chunks + LEAD, LEAD % 2, 0, rows + early_rows, LEAD - 1, (attend_local,), (pick_docs,)
+        )
+        send_docs(LEAD - 1)
+        refill(jnp.int32(n_chunks + LEAD))
+        keep_heads(2)
         kv_remote(2).wait()
     with mark("PH_both"):
         def both(j, carry):
@@ -676,7 +696,6 @@
                 (attend_local, attend_early), (pick_docs, keep_early),
             )
             send_docs(j - 1)
-            store_early(j - 1)
             refill(n_chunks + j)
             return carry
 
@@ -687,19 +706,16 @@
             (attend_local, attend_early), (pick_docs, keep_early),
         )
         send_docs(n_chunks - 1)
-        store_early(n_chunks - 1)
     with mark("PJ_early"):
         def behind(j, carry):
             step(
                 1, total - LEAD + j, lax.rem(j, 2), rows, early_rows, j - 1,
                 (attend_early,), (keep_early,),
             )
-            store_early(j - 1)
             return carry
 
         lax.fori_loop(1, LEAD, behind, 0)
         last_step(LEAD - 1, (attend_early,), (keep_early,))
-        store_early(LEAD - 1)
     with mark("PK_sends"):
         for j in range(n_chunks):
             h_remote(j).wait_send()
@@ -707,12 +723,15 @@
             early_forward(j).wait_send()
             for k in range(half):
                 early_remote(k, j).wait_send()
-        for slot in range(half):
-            early_stored(slot).wait()
-        own_stored().wait()
     with mark("PL_docs"):
         for k in range(1, len(late_masks)):
             doc_all(k).wait()
+
+
+def put_out(held, out, sem):
+    copy = pltpu.make_async_copy(held, out, sem)
+    copy.start()
+    copy.wait()
 
 
 def fused_device(sizes, hidden, doc_lengths, doc_target, norm_gain, q_weight, kv_weight):
@@ -735,18 +754,19 @@
     early_blocks = vmem((n_chunks, early_rows, CHUNK), bf16)
     result = pl.pallas_call(
         functools.partial(fused_kernel, sizes),
-        out_shape=jax.ShapeDtypeStruct((n_dp * capacity, width), bf16),
+        out_shape=vmem((n_dp * capacity, width), bf16),
         in_specs=[
             pl.BlockSpec(memory_space=pl.ANY),
-            pl.BlockSpec(memory_space=pltpu.VMEM),
-            pl.BlockSpec(memory_space=pltpu.VMEM),
-            pl.BlockSpec(memory_space=pltpu.VMEM),
+            pl.BlockSpec(memory_space=pl.ANY),
+            pl.BlockSpec(memory_space=pl.ANY),
+            pl.BlockSpec(memory_space=pl.ANY),
             pl.BlockSpec(memory_space=pl.ANY),
             pl.BlockSpec(memory_space=pl.ANY),
         ],
-        out_specs=pl.BlockSpec(memory_space=pl.ANY),
+        out_specs=pl.BlockSpec(memory_space=vmem),
         scratch_shapes=[
             vmem((8, 128), jnp.int32),
+            vmem((1, docs), jnp.int32), vmem((1, docs), jnp.int32), vmem((1, features), jnp.float32),
             blocks, blocks, blocks, blocks, blocks, early_blocks, early_blocks,
             vmem((n_chunks, half, capacity, CHUNK), bf16),
             vmem((8, 128), jnp.int32),
@@ -755,6 +775,7 @@
             vmem((most, features), bf16),
             vmem((n_kv, n_kv), bf16),
             vmem((most, n_kv), jnp.float32),
+            vmem((most, n_kv), bf16),
             vmem((most, CHUNK), jnp.float32),
             vmem((most, CHUNK), jnp.float32),
             vmem((STEPS, own_kv, most, HD), bf16),
@@ -767,20 +788,27 @@
             vmem((early_rows, rows), bf16),
             vmem((n_late * capacity, rows), bf16),
             vmem((2, most, CHUNK), bf16),
+            vmem((rows, CHUNK), jnp.float32),
             vmem((n_late, capacity, width), bf16),
-            vmem((half, capacity, width), bf16),
             dma((n_chunks,)), dma((n_chunks,)), dma((n_chunks,)), dma, dma,
             dma((features // KV_ROWS,)), dma((SLOTS,)), dma((STEPS + 1,)), dma((STEPS + 1,)),
             dma((n_chunks,)), dma((n_chunks,)), dma((n_chunks,)), dma((n_chunks,)),
-            dma((n_late,)), dma((n_late,)), dma((half + 1,)),
+            dma((n_late,)), dma((n_late,)),
             dma((half, n_chunks)), dma((half, n_chunks)), dma((n_chunks,)), dma((n_chunks,)),
-            dma((half,)), dma((half,)),
+            dma((half,)), dma((half,)), dma((3,)),
         ],
         compiler_params=pltpu.CompilerParams(
-            collective_id=0, has_side_effects=True, vmem_limit_bytes=67043328
+            collective_id=0, has_side_effects=True, vmem_limit_bytes=64800000
         ),
     )(hidden[0], doc_lengths[0], doc_target[0], norm_gain, q_weight[0], kv_weight[0])
-    return result[None]
+    return pl.pallas_call(
+        put_out,
+        out_shape=jax.ShapeDtypeStruct((n_dp * capacity, width), bf16),
+        in_specs=[pl.BlockSpec(memory_space=vmem)],
+        out_specs=pl.BlockSpec(memory_space=pl.ANY),
+        scratch_shapes=[dma],
+        compiler_params=pltpu.CompilerParams(vmem_limit_bytes=4194304),
+    )(result)[None]
 
 
 def solution(mesh):

time: 76.5 us -> 71.4 us (0.933)
  local copies, waits for them, and re-layouts: 3.13 us -> 0 us
  Pallas kernels: 73.1 us -> 71.1 us
    unnamed x1 -> x0, local copies, waits for them, and re-layouts: 3.13 us -> none
    pallas_call x1 -> x2, Pallas kernels: 73.1 us -> 71.1 us  [the longest x1 69.7 us: fused_device(): pl.pallas_call(functools.partial(fused_kernel, sizes), out_shape=vmem((n_...]
where the time goes in v3:
time: 71.4 us; the launch traced here: 71.2 us
  Pallas kernels  71.1 us (100%)
    pallas_call x1, Pallas kernels, fused_device(): pl.pallas_call(functools.partial(fused_kernel, sizes), out_shape=vmem((n_...  69.7 us

profile of v3, /device:TPU:0, one launch (start us, length us, event | category | flops | bytes accessed | tf_op | source)
XLA Modules:
  0.0 71.2 jit_solution(14729355798354188073)
XLA Ops:
  0.0 69.7 %shard_map.64.held = bf16[256,4096]{1,0:T(8,128)(2,1)S(1)} custom-call(bf16[128,4096]{1,0:T(8,128)(2,1)} %bitcast.7, s32[1,8]{1,0:T(1,128)} %bitcast.8, s32[1,8]{1,0:T(1,128)} %bitcast.9, f32[1,8192]{1,0:T(1,128)} %gain_in.1, bf16[8192,4096]{1,0:T(8,128)(2,1)} %bitcast.3.wq, bf16[8192,1024]{1,0:T(8,128)(2,1)} %bitcast.6), custom_call_target="tpu_custom_call" | custom-call | tf_op jit(solution)/shard_map/pallas_call | solution.py:755
  69.7 1.3 %shard_map.65 = bf16[256,4096]{1,0:T(8,128)(2,1)} custom-call(bf16[256,4096]{1,0:T(8,128)(2,1)S(1)} %shard_map.64.held), custom_call_target="tpu_custom_call" | custom-call | tf_op jit(solution)/shard_map/pallas_call | solution.py:804

commit v4 on v3

--- a/solution.py
+++ b/solution.py
@@ -182,9 +182,9 @@
     def x_copy(j):
         return pltpu.make_async_copy(hidden.at[:, cols(j)], x_own.at[j], sem_x.at[j])
 
-    def x_remote(j):
-        return pltpu.make_async_remote_copy(
-            x_own.at[j], x_other.at[j], sem_xs.at[j], sem_xr.at[j],
+    def x_remote():
+        return pltpu.make_async_remote_copy(
+            x_own, x_other, sem_xs, sem_xr,
             device_id={"tensor": other}, device_id_type=pl.DeviceIdType.MESH,
         )
 
@@ -203,13 +203,13 @@
     def early_remote(k, j):
         return pltpu.make_async_remote_copy(
             early_send.at[j, k], early_own.at[j, k * capacity:(k + 1) * capacity],
-            sem_es.at[k, j], sem_er.at[k, j],
+            sem_es.at[k], sem_er.at[k, j],
             device_id={"dp": early_partners[k]}, device_id_type=pl.DeviceIdType.MESH,
         )
 
     def early_forward(j):
         return pltpu.make_async_remote_copy(
-            early_own.at[j], early_other.at[j], sem_gs.at[j], sem_gr.at[j],
+            early_own.at[j], early_other.at[j], sem_gs, sem_gr.at[j],
             device_id={"tensor": other}, device_id_type=pl.DeviceIdType.MESH,
         )
 
@@ -226,13 +226,13 @@
 
     def h_remote(j):
         return pltpu.make_async_remote_copy(
-            h_send.at[j], next_own.at[j], sem_hs.at[j], sem_hr.at[j],
+            h_send.at[j], next_own.at[j], sem_hs, sem_hr.at[j],
             device_id={"pipe": following}, device_id_type=pl.DeviceIdType.MESH,
         )
 
     def forward_remote(j):
         return pltpu.make_async_remote_copy(
-            next_own.at[j], next_other.at[j], sem_fs.at[j], sem_fr.at[j],
+            next_own.at[j], next_other.at[j], sem_fs, sem_fr.at[j],
             device_id={"tensor": other}, device_id_type=pl.DeviceIdType.MESH,
         )
 
@@ -600,7 +600,7 @@
     with mark("P1_xsend"):
         for j in range(n_chunks):
             x_copy(j).wait()
-            x_remote(j).start()
+        x_remote().start()
     meta_remote().start()
     for c in range(SLOTS):
         ring_copy(c).start()
@@ -608,8 +608,7 @@
         absorb_half(x_own, side)
         multiply_half(0)
     with mark("P3_xwait"):
-        for j in range(n_chunks):
-            x_remote(j).wait()
+        x_remote().wait()
     with mark("P4_other"):
         absorb_half(x_other, other)
         multiply_half(1)
@@ -717,12 +716,21 @@
         lax.fori_loop(1, LEAD, behind, 0)
         last_step(LEAD - 1, (attend_early,), (keep_early,))
     with mark("PK_sends"):
-        for j in range(n_chunks):
-            h_remote(j).wait_send()
-            forward_remote(j).wait_send()
-            early_forward(j).wait_send()
-            for k in range(half):
-                early_remote(k, j).wait_send()
+        for held, there, sent, got in (
+            (h_send, next_own, sem_hs, sem_hr.at[0]),
+            (next_own, next_other, sem_fs, sem_fr.at[0]),
+            (early_own, early_other, sem_gs, sem_gr.at[0]),
+        ):
+            whom = {"pipe": following} if held is h_send else {"tensor": other}
+            pltpu.make_async_remote_copy(
+                held, there, sent, got, device_id=whom, device_id_type=pl.DeviceIdType.MESH
+            ).wait_send()
+        for k in range(half):
+            pltpu.make_async_remote_copy(
+                early_send.at[:, k], early_own.at[:, k * capacity:(k + 1) * capacity],
+                sem_es.at[k], sem_er.at[k, 0],
+                device_id={"dp": early_partners[k]}, device_id_type=pl.DeviceIdType.MESH,
+            ).wait_send()
     with mark("PL_docs"):
         for k in range(1, len(late_masks)):
             doc_all(k).wait()
@@ -790,11 +798,11 @@
             vmem((2, most, CHUNK), bf16),
             vmem((rows, CHUNK), jnp.float32),
             vmem((n_late, capacity, width), bf16),
-            dma((n_chunks,)), dma((n_chunks,)), dma((n_chunks,)), dma, dma,
+            dma((n_chunks,)), dma, dma, dma, dma,
             dma((features // KV_ROWS,)), dma((SLOTS,)), dma((STEPS + 1,)), dma((STEPS + 1,)),
-            dma((n_chunks,)), dma((n_chunks,)), dma((n_chunks,)), dma((n_chunks,)),
+            dma, dma((n_chunks,)), dma, dma((n_chunks,)),
             dma((n_late,)), dma((n_late,)),
-            dma((half, n_chunks)), dma((half, n_chunks)), dma((n_chunks,)), dma((n_chunks,)),
+            dma((half,)), dma((half, n_chunks)), dma, dma((n_chunks,)),
             dma((half,)), dma((half,)), dma((3,)),
         ],
         compiler_params=pltpu.CompilerParams(

time: 71.4 us -> 70.4 us (0.986)
  Pallas kernels: 71.1 us -> 70.1 us
    pallas_call x1, Pallas kernels: 69.7 us -> 68.8 us  [fused_device(): pl.pallas_call(functools.partial(fused_kernel, sizes), out_shape=vmem((n_...]
where the time goes in v4:
time: 70.4 us; the launch traced here: 70.3 us
  Pallas kernels  70.1 us (100%)
    pallas_call x1, Pallas kernels, fused_device(): pl.pallas_call(functools.partial(fused_kernel, sizes), out_shape=vmem((n_...  68.8 us

profile of v4, /device:TPU:0, one launch (start us, length us, event | category | flops | bytes accessed | tf_op | source)
XLA Modules:
  0.0 70.3 jit_solution(16726385181287888308)
XLA Ops:
  0.0 68.8 %shard_map.64.held = bf16[256,4096]{1,0:T(8,128)(2,1)S(1)} custom-call(bf16[128,4096]{1,0:T(8,128)(2,1)} %bitcast.7, s32[1,8]{1,0:T(1,128)} %bitcast.8, s32[1,8]{1,0:T(1,128)} %bitcast.9, f32[1,8192]{1,0:T(1,128)} %gain_in.1, bf16[8192,4096]{1,0:T(8,128)(2,1)} %bitcast.3.wq, bf16[8192,1024]{1,0:T(8,128)(2,1)} %bitcast.6), custom_call_target="tpu_custom_call" | custom-call | tf_op jit(solution)/shard_map/pallas_call | solution.py:763
  68.8 1.3 %shard_map.65 = bf16[256,4096]{1,0:T(8,128)(2,1)} custom-call(bf16[256,4096]{1,0:T(8,128)(2,1)S(1)} %shard_map.64.held), custom_call_target="tpu_custom_call" | custom-call | tf_op jit(solution)/shard_map/pallas_call | solution.py:812

commit v5 on v4

--- a/solution.py
+++ b/solution.py
@@ -473,14 +473,14 @@
             product = part if product is None else product + part
         return product
 
-    def begin_query(c):
-        ring_copy(c).wait()
-        begun[...] = query_part(c, 0, early_deep)
-
-    def end_query(c):
-        product = begun[...] + query_part(c, early_deep, width)
-        q_held[0, 0:rows] = (product * scales[0:rows]).astype(jnp.bfloat16)
-        refill(jnp.int32(c))
+    def begin_query(j):
+        ring_copy(n_chunks + j).wait()
+        begun[j] = query_part(n_chunks + j, 0, early_deep)
+
+    def end_query(j):
+        product = begun[j] + query_part(n_chunks + j, early_deep, width)
+        q_held[j, 0:rows] = (product * scales[0:rows]).astype(jnp.bfloat16)
+        refill(jnp.int32(n_chunks + j))
 
     def step(layer, c, slot, first, count, before, attends, settles, extras=()):
         ring_copy(c).wait()
@@ -648,22 +648,27 @@
             forward_remote(j - 1).wait_recv()
             absorb_local(j - 1)
             if j == n_chunks - lag + 1:
-                begin_query(n_chunks)
+                begin_query(0)
             for _ in range(2):
                 if gone < j - 4:
                     pass_early(gone)
                     early_forward(gone - 1).wait_recv()
                     absorb_early(gone - 1)
                     gone += 1
+            if j == n_chunks - 2:
+                begin_query(1)
     with mark("PD_last"):
         forward_remote(n_chunks - 1).wait_recv()
         absorb_local(n_chunks - 1)
     with mark("PE_kv"):
         keys_values(1)
     with mark("PF_first"):
-        end_query(n_chunks)
+        end_query(0)
         keep_heads(1)
+        end_query(1)
         kv_remote(1).wait()
+        last_step(0, (attend_local,), (pick_docs,))
+        send_docs(0)
     with mark("PG_local"):
         def local(j, carry):
             step(
@@ -673,7 +678,7 @@
             refill(n_chunks + j)
             return carry
 
-        lax.fori_loop(1, LEAD - 1, local, 0)
+        lax.fori_loop(2, LEAD - 1, local, 0)
         for i in range(gone, n_chunks):
             pass_early(i)
         lax.fori_loop(LEAD - 1, LEAD, local, 0)
@@ -796,7 +801,7 @@
             vmem((early_rows, rows), bf16),
             vmem((n_late * capacity, rows), bf16),
             vmem((2, most, CHUNK), bf16),
-            vmem((rows, CHUNK), jnp.float32),
+            vmem((2, rows, CHUNK), jnp.float32),
             vmem((n_late, capacity, width), bf16),
             dma((n_chunks,)), dma, dma, dma, dma,
             dma((features // KV_ROWS,)), dma((SLOTS,)), dma((STEPS + 1,)), dma((STEPS + 1,)),

time: 70.4 us -> 70 us (level)
  no operation moved by 1% of the time
where the time goes in v5:
time: 70 us; the launch traced here: 69.9 us
  Pallas kernels  69.7 us (100%)
    pallas_call x1, Pallas kernels, fused_device(): pl.pallas_call(functools.partial(fused_kernel, sizes), out_shape=vmem((n_...  68.4 us

profile of v5, /device:TPU:0, one launch (start us, length us, event | category | flops | bytes accessed | tf_op | source)
XLA Modules:
  0.0 69.9 jit_solution(12856303793228886888)
XLA Ops:
  0.0 68.4 %shard_map.64.held = bf16[256,4096]{1,0:T(8,128)(2,1)S(1)} custom-call(bf16[128,4096]{1,0:T(8,128)(2,1)} %bitcast.7, s32[1,8]{1,0:T(1,128)} %bitcast.8, s32[1,8]{1,0:T(1,128)} %bitcast.9, f32[1,8192]{1,0:T(1,128)} %gain_in.1, bf16[8192,4096]{1,0:T(8,128)(2,1)} %bitcast.3.wq, bf16[8192,1024]{1,0:T(8,128)(2,1)} %bitcast.6), custom_call_target="tpu_custom_call" | custom-call | tf_op jit(solution)/shard_map/pallas_call | solution.py:768
  68.4 1.3 %shard_map.65 = bf16[256,4096]{1,0:T(8,128)(2,1)} custom-call(bf16[256,4096]{1,0:T(8,128)(2,1)S(1)} %shard_map.64.held), custom_call_target="tpu_custom_call" | custom-call | tf_op jit(solution)/shard_map/pallas_call | solution.py:817

commit v6 on v5

--- a/solution.py
+++ b/solution.py
@@ -180,7 +180,7 @@
         )
 
     def x_copy(j):
-        return pltpu.make_async_copy(hidden.at[:, cols(j)], x_own.at[j], sem_x.at[j])
+        return pltpu.make_async_copy(hidden.at[:, cols(j)], x_own.at[j], sem_x)
 
     def x_remote():
         return pltpu.make_async_remote_copy(
@@ -203,7 +203,7 @@
     def early_remote(k, j):
         return pltpu.make_async_remote_copy(
             early_send.at[j, k], early_own.at[j, k * capacity:(k + 1) * capacity],
-            sem_es.at[k], sem_er.at[k, j],
+            sem_es.at[k], sem_er.at[j],
             device_id={"dp": early_partners[k]}, device_id_type=pl.DeviceIdType.MESH,
         )
 
@@ -537,8 +537,10 @@
         absorb_next(early_own, early_other, rows, early_rows, chunks)
 
     def pass_early(j):
-        for k in range(half):
-            early_remote(k, j).wait_recv()
+        pltpu.make_async_remote_copy(
+            normed_next.at[rows:rows + early_rows, 0:CHUNK], early_own.at[j], sem_es.at[0], sem_er.at[j],
+            device_id={"dp": early_partners[0]}, device_id_type=pl.DeviceIdType.MESH,
+        ).wait_recv()
         early_forward(j).start()
 
     def pick_docs(j, done):
@@ -598,8 +600,7 @@
     with mark("PX_barrier"):
         pl.semaphore_wait(barrier, greeted)
     with mark("P1_xsend"):
-        for j in range(n_chunks):
-            x_copy(j).wait()
+        pltpu.make_async_copy(h_send, x_own, sem_x).wait()
         x_remote().start()
     meta_remote().start()
     for c in range(SLOTS):
@@ -733,7 +734,7 @@
         for k in range(half):
             pltpu.make_async_remote_copy(
                 early_send.at[:, k], early_own.at[:, k * capacity:(k + 1) * capacity],
-                sem_es.at[k], sem_er.at[k, 0],
+                sem_es.at[k], sem_er.at[0],
                 device_id={"dp": early_partners[k]}, device_id_type=pl.DeviceIdType.MESH,
             ).wait_send()
     with mark("PL_docs"):
@@ -803,11 +804,11 @@
             vmem((2, most, CHUNK), bf16),
             vmem((2, rows, CHUNK), jnp.float32),
             vmem((n_late, capacity, width), bf16),
-            dma((n_chunks,)), dma, dma, dma, dma,
+            dma, dma, dma, dma, dma,
             dma((features // KV_ROWS,)), dma((SLOTS,)), dma((STEPS + 1,)), dma((STEPS + 1,)),
             dma, dma((n_chunks,)), dma, dma((n_chunks,)),
             dma((n_late,)), dma((n_late,)),
-            dma((half,)), dma((half, n_chunks)), dma, dma((n_chunks,)),
+            dma((half,)), dma((n_chunks,)), dma, dma((n_chunks,)),
             dma((half,)), dma((half,)), dma((3,)),
         ],
         compiler_params=pltpu.CompilerParams(

time: 70 us -> 69.7 us (level)
  no operation moved by 1% of the time
where the time goes in v6:
time: 69.7 us; the launch traced here: 69.6 us
  Pallas kernels  69.4 us (100%)
    pallas_call x1, Pallas kernels, fused_device(): pl.pallas_call(functools.partial(fused_kernel, sizes), out_shape=vmem((n_...  68.1 us

profile of v6, /device:TPU:0, one launch (start us, length us, event | category | flops | bytes accessed | tf_op | source)
XLA Modules:
  0.0 69.6 jit_solution(10245566096337601162)
XLA Ops:
  0.0 68.1 %shard_map.64.held = bf16[256,4096]{1,0:T(8,128)(2,1)S(1)} custom-call(bf16[128,4096]{1,0:T(8,128)(2,1)} %bitcast.7, s32[1,8]{1,0:T(1,128)} %bitcast.8, s32[1,8]{1,0:T(1,128)} %bitcast.9, f32[1,8192]{1,0:T(1,128)} %gain_in.1, bf16[8192,4096]{1,0:T(8,128)(2,1)} %bitcast.3.wq, bf16[8192,1024]{1,0:T(8,128)(2,1)} %bitcast.6), custom_call_target="tpu_custom_call" | custom-call | tf_op jit(solution)/shard_map/pallas_call | solution.py:769
  68.1 1.3 %shard_map.65 = bf16[256,4096]{1,0:T(8,128)(2,1)} custom-call(bf16[256,4096]{1,0:T(8,128)(2,1)S(1)} %shard_map.64.held), custom_call_target="tpu_custom_call" | custom-call | tf_op jit(solution)/shard_map/pallas_call | solution.py:818
